TPU v7x, 32 devices: a whole 2x2x4 slice. The times are simulated.
32 devices in a mesh: clip: 4 (over x, core), tm: 8 (over z, y).
Axes of the slice: x: 2, y: 2, z: 4, core: 2. Of those that a mesh axis runs over, the one named last changes fastest.
Arguments:
- inputs: bfloat16 [4, 2560, 768], P('clip', 'tm'), may hold values from -6 to 6
- query_states: bfloat16 [4, 2560, 768], P('clip', 'tm'), may hold values from -9 to 9
- key_states: bfloat16 [4, 2560, 768], P('clip', 'tm'), may hold values from -9 to 9
- value_states: bfloat16 [4, 2560, 768], P('clip', 'tm'), may hold values from -6 to 6
- out_grad: bfloat16 [4, 2560, 768], P('clip', 'tm'), may hold values from -1.1953125 to 1.1953125
- first_flags: int32 [4, 8], P('clip'), may hold values from 0 to 1, as said below
- weight: float32 [768, 768], P('tm'), may hold values from -1.2 to 1.2
- moment_one: float32 [768, 768], P('tm'), may hold values from -6 to 6
- moment_two: float32 [768, 768], P('tm'), may hold values from 0.25 to 4
Outputs:
- new_weight: float32 [768, 768], P('tm')
- new_moment_one: float32 [768, 768], P('tm')
- new_moment_two: float32 [768, 768], P('tm')
Inputs may be any that keep to these rules, and one draw needn't show every extreme that they name: `first_flags`: the first frame of every sequence has flag 1.
All inputs are finite; a program needn't handle non-finite values.
Results may differ from a plain program's by a relative error of at most 0.0044.
Values may be sent and summed in bfloat16 or wider, within the bound.
No kernel may reach another device: no remote copies, remote signals or barrier semaphores. Data moves between devices by JAX's collectives and lax.ppermute only.
A program may use at most 64 MiB of HBM per device.

v0:
```python
import functools
import math

import jax
import jax.numpy as jnp
from jax import lax
from jax.experimental import pallas as pl
from jax.experimental.pallas import tpu as pltpu
from jax.sharding import Mesh, PartitionSpec as P


HEAD_DIM = 128


beta_one = 0.9
beta_two = 0.95
learn_rate = 0.001
adam_eps = 1e-08
decay_rate = 0.1
step_count = 10.0

TOKENS_BOTH = (((1,), (1,)), ((), ()))


def adamw(weight, moment_one, moment_two, gradient):
    new_one = beta_one * moment_one + (1.0 - beta_one) * gradient
    new_two = beta_two * moment_two + (1.0 - beta_two) * gradient * gradient
    corr_one = new_one / (1.0 - beta_one**step_count)
    corr_two = new_two / (1.0 - beta_two**step_count)
    new_weight = weight - learn_rate * (
        corr_one / (jnp.sqrt(corr_two) + adam_eps) + decay_rate * weight
    )
    return (new_weight, new_one, new_two)


def near_by(value):
    return pltpu.with_memory_space_constraint(value, pltpu.VMEM)


def far_off(value):
    return pltpu.with_memory_space_constraint(value, pltpu.HBM)


def cut_kernel(spans, *refs):
    wholes, outs, sem = refs[: len(spans)], refs[len(spans) : -1], refs[-1]
    copies, index = [], 0
    for whole, rows in zip(wholes, spans):
        for start, size in rows:
            copies.append(
                pltpu.make_async_copy(whole.at[pl.ds(start, size)], outs[index], sem.at[index])
            )
            index += 1
    for copy in copies:
        copy.start()
    for copy in copies:
        copy.wait()


def cut_out(wholes, spans):
    anywhere = pl.BlockSpec(memory_space=pl.ANY)
    shapes = [
        jax.ShapeDtypeStruct((size, whole.shape[1]), whole.dtype)
        for whole, rows in zip(wholes, spans)
        for _, size in rows
    ]
    return pl.pallas_call(
        functools.partial(cut_kernel, spans),
        in_specs=[anywhere] * len(wholes),
        out_specs=[pl.BlockSpec(memory_space=pltpu.VMEM)] * len(shapes),
        out_shape=shapes,
        scratch_shapes=[pltpu.SemaphoreType.DMA((len(shapes),))],
        compiler_params=pltpu.CompilerParams(vmem_limit_bytes=4 << 20),
        name="cut_out",
    )(*[far_off(whole) for whole in wholes])


def pick_kernel(start, far, whole, out, sem):
    side = lax.axis_index("side")

    @pl.when(side == 1)
    def _():
        copy = pltpu.make_async_copy(far, out, sem)
        copy.start()
        copy.wait()

    @pl.when(side != 1)
    def _():
        copy = pltpu.make_async_copy(whole.at[pl.ds(start, out.shape[0])], out, sem)
        copy.start()
        copy.wait()


def picked(far, whole, start):
    anywhere = pl.BlockSpec(memory_space=pl.ANY)
    return pl.pallas_call(
        functools.partial(pick_kernel, start),
        in_specs=[anywhere, anywhere],
        out_specs=pl.BlockSpec(memory_space=pltpu.VMEM),
        out_shape=jax.ShapeDtypeStruct(far.shape, far.dtype),
        scratch_shapes=[pltpu.SemaphoreType.DMA],
        compiler_params=pltpu.CompilerParams(vmem_limit_bytes=1 << 20),
        name="picked",
    )(far, far_off(whole))


def frame_index():
    return lax.axis_index("hop") * lax.axis_size("side") + lax.axis_index("side")


def folded(value):
    return value.reshape(value.shape[0] // 8, 8, value.shape[1])


def head_columns(refs, head):
    columns = slice(head * HEAD_DIM, (head + 1) * HEAD_DIM)
    parts = [ref[:, columns] for ref in refs]
    return parts[0] if len(parts) == 1 else jnp.concatenate(parts, axis=0)


def key_grads_kernel(key_cuts, val_cuts, flags, query, grad, *refs):
    keys, refs = refs[:key_cuts], refs[key_cuts:]
    values, refs = refs[:val_cuts], refs[val_cuts:]
    out, *scratch = refs
    scores, dprobs, raiseds, dscores = (scratch[i : i + 2] for i in (0, 2, 4, 6))
    rows, width = query.shape
    heads = width // HEAD_DIM
    lanes = scores[0].shape[1]
    scaling = 1.0 / math.sqrt(HEAD_DIM)
    power = scaling * math.log2(math.e)
    position = frame_index()
    near_ok = jnp.logical_and(position >= 1, flags[0, position] == 0)
    far_ok = jnp.logical_and(
        jnp.logical_and(near_ok, position >= 2), flags[0, jnp.maximum(position - 1, 0)] == 0
    )
    seen = (None, far_ok, near_ok)
    blank = jnp.zeros((lanes - rows, HEAD_DIM), query.dtype)
    step = 32 if rows % 32 == 0 else rows
    base = pl.multiple_of(jnp.minimum(flags[0, 0], 0) * 32, 32)

    def piece_of(start, size=step):
        return pl.ds(base + start, size)

    def padded(ref, head):
        return jnp.concatenate([head_columns([ref], head), blank], axis=0)

    def products(head):
        slot = head % 2
        for refs_of, other, target in ((keys, query, scores), (values, grad, dprobs)):
            target[slot][piece_of(0, 3 * rows), :] = lax.dot_general(
                head_columns(refs_of, head),
                padded(other, head),
                TOKENS_BOTH,
                preferred_element_type=jnp.float32,
            )

    def softmax(head):
        slot = head % 2
        tops = []
        for frame, ok in enumerate(seen):
            top = jnp.max(folded(scores[slot][piece_of(frame * rows, rows), :]), axis=0)
            tops.append(top if ok is None else jnp.where(ok, top, -jnp.inf))
        top = jnp.max(functools.reduce(jnp.maximum, tops), axis=0, keepdims=True) * power
        total = dots = 0.0
        for frame, ok in enumerate(seen):
            lift = top if ok is None else jnp.where(ok, top, jnp.inf)
            for start in range(frame * rows, (frame + 1) * rows, step):
                piece = piece_of(start)
                raised = jnp.exp2(scores[slot][piece, :] * power - lift)
                raiseds[slot][piece, :] = raised
                total = total + jnp.sum(folded(raised), axis=0)
                dots = dots + jnp.sum(folded(raised * dprobs[slot][piece, :]), axis=0)
        inverse = 1.0 / jnp.sum(total, axis=0, keepdims=True)
        delta = jnp.sum(dots, axis=0, keepdims=True) * inverse
        level = inverse * scaling
        for start in range(0, 3 * rows, step):
            piece = piece_of(start)
            value = raiseds[slot][piece, :] * level * (dprobs[slot][piece, :] - delta)
            dscores[slot][piece, :] = value.astype(dscores[slot].dtype)

    def collect(head):
        part = jnp.dot(
            dscores[head % 2][piece_of(0, 3 * rows), :],
            padded(query, head),
            preferred_element_type=jnp.float32,
        )
        out[:, head * HEAD_DIM : (head + 1) * HEAD_DIM] = part.astype(out.dtype)

    for beat in range(heads + 2):
        if beat >= 2:
            collect(beat - 2)
        if beat < heads:
            products(beat)
        if 1 <= beat <= heads:
            softmax(beat - 1)


def key_grads(flag_row, queries, grads, keys, values):
    rows, width = queries.shape
    lanes = pl.cdiv(rows, 128) * 128
    smem = pl.BlockSpec(memory_space=pltpu.SMEM)
    vmem = pl.BlockSpec(memory_space=pltpu.VMEM)
    arrays = [near_by(a) for a in (queries, grads, *keys, *values)]
    return pl.pallas_call(
        functools.partial(key_grads_kernel, len(keys), len(values)),
        in_specs=[smem] + [vmem] * len(arrays),
        out_specs=vmem,
        out_shape=pltpu.VMEM((3 * rows, width), jnp.bfloat16),
        scratch_shapes=[
            pltpu.VMEM((3 * rows, lanes), dtype)
            for dtype in (jnp.float32, jnp.float32, jnp.float32, jnp.bfloat16)
            for _ in range(2)
        ],
        compiler_params=pltpu.CompilerParams(vmem_limit_bytes=24 << 20),
        name="key_grads",
    )(flag_row, *arrays)


def turn_kernel(*refs):
    *values, out = refs
    out[...] = jnp.concatenate([v[...] for v in values], axis=0).T


def turned(*values):
    vmem = pl.BlockSpec(memory_space=pltpu.VMEM)
    tokens = sum(v.shape[0] for v in values)
    return pl.pallas_call(
        turn_kernel,
        in_specs=[vmem] * len(values),
        out_specs=vmem,
        out_shape=pltpu.VMEM((values[0].shape[1], tokens), values[0].dtype),
        compiler_params=pltpu.CompilerParams(vmem_limit_bytes=16 << 20),
        name="turned",
    )(*[near_by(v) for v in values])


def gradient_kernel(steps, wanted, early, last, parts, *refs):
    outs = refs[: len(wanted)]
    place, hops = lax.axis_index("hop"), lax.axis_size("hop")
    core = lax.axis_index("core")
    _, pairs, rows, half = outs[0].shape
    span = pairs * rows
    blocks = []
    for step in steps:
        here = pl.ds(pl.multiple_of(((place + step) % hops) * span, span), span)
        blocks.append(jnp.concatenate([early[here, :], last[here, :]], axis=1))
    features = jnp.concatenate(blocks, axis=0)
    if len(wanted) > 1:
        whole = refs[-1]
        whole[...] = jnp.dot(features, parts[...], preferred_element_type=jnp.float32)
    for name, target in zip(wanted, outs):
        side = core if name == "kept" else 1 - core
        columns = pl.ds(pl.multiple_of(side * half, 128), half)
        if len(wanted) == 1:
            total = jnp.dot(features, parts[:, columns], preferred_element_type=jnp.float32)
        for index in range(len(steps)):
            for pair in range(pairs):
                start = (index * pairs + pair) * rows
                lines = slice(start, start + rows)
                value = total[lines] if len(wanted) == 1 else whole[lines, columns]
                target[index, pair] = value.astype(target.dtype)


def partial_gradient(steps, wanted, frames, early, last, parts):
    vmem = pl.BlockSpec(memory_space=pltpu.VMEM)
    features, width = early.shape[0], parts.shape[1]
    rows = features // frames
    pairs = lax.axis_size("side")
    shape = (len(steps), pairs, rows, width // 2)
    kinds = {"kept": jnp.float32, "sent": jnp.bfloat16}
    scratch = [pltpu.VMEM((len(steps) * pairs * rows, width), jnp.float32)]
    return pl.pallas_call(
        functools.partial(gradient_kernel, steps, wanted),
        in_specs=[vmem] * 3,
        out_specs=[vmem] * len(wanted),
        out_shape=[pltpu.VMEM(shape, kinds[name]) for name in wanted],
        scratch_shapes=scratch if len(wanted) > 1 else [],
        compiler_params=pltpu.CompilerParams(vmem_limit_bytes=24 << 20),
        name="partial_gradient",
    )(*[near_by(a) for a in (early, last, parts)])


def body(
    inputs,
    query_states,
    key_states,
    value_states,
    out_grad,
    first_flags,
    weight,
    moment_one,
    moment_two,
):
    hops, pairs = lax.axis_size("hop"), lax.axis_size("side")
    frames = hops * pairs
    swap = [(0, 1), (1, 0)]

    own = (key_states[0], value_states[0], inputs[0])
    tokens = own[0].shape[0]
    cut = tokens * 9 // 20 // 16 * 16
    spans = ((0, cut), (cut, tokens - cut))
    first = cut_out(own[:1], (spans[:1],))
    pieces = [*first, *cut_out(own, (spans[1:], spans, spans))]

    def behind(value, index):
        far = lax.ppermute(value, ("hop", "side"), [(i, i + 2) for i in range(frames - 2)])
        mixed = picked(far, own[index // 2], spans[index % 2][0])
        near = lax.ppermute(mixed, "side", swap)
        return far, near

    moved = [behind(piece, index) for index, piece in enumerate(pieces)]
    keys, values, features = (
        (whole, *zip(*moved[2 * i : 2 * i + 2])) for i, whole in enumerate(own)
    )
    early = turned(features[0], *features[1])
    parts = key_grads(
        first_flags,
        query_states[0],
        out_grad[0],
        (keys[0], *keys[1], *keys[2]),
        (values[0], *values[1], *values[2]),
    )
    last = turned(*features[2])
    stays, comes = [], []
    for steps, name in zip(groups_of(hops), STREAM):
        product = functools.partial(partial_gradient, steps)
        window = (frames, early, last, parts)
        if name == STREAM[0]:
            (sent,), (kept,) = product(("sent",), *window), product(("kept",), *window)
        else:
            kept, sent = product(("kept", "sent"), *window)
        taken = lax.ppermute(sent, "core", swap)
        kept, sent = by_side(kept, taken)
        taken = lax.ppermute(sent, "side", swap)
        send_on(steps, kept, taken, stays, comes)
    mine = small_call(add_kernel, *stays, *comes, out=thin(stays[0].shape))
    own, other = over_clip(mine, swap)
    state = (weight, moment_one, moment_two)
    outs = update_columns("own", own, state)
    return update_columns("other", other, state, outs)


def groups_of(hops):
    if hops > 4:
        return (tuple(range(hops)),)
    order = (*sorted(range(1, hops), key=lambda k: -min(k, hops - k)), 0)
    return tuple(group for group in (order[: hops // 2], order[hops // 2 :]) if group)


def send_on(steps, kept, taken, stays, comes):
    hops = lax.axis_size("hop")
    _, rows, half = kept.shape
    if hops > 4:
        kernel = functools.partial(line_kernel, steps)
        line = small_call(kernel, kept, taken, out=thin(kept.shape))
        stays.extend(lax.all_to_all(line, "hop", 0, 0))
        return
    outs = tuple(thin((rows, half)) if step else wide((rows, half)) for step in steps)
    blocks = small_call(by_hop_kernel, kept, taken, out=outs)
    for step, block in zip(steps, blocks):
        if step:
            route = [(i, (i + step) % hops) for i in range(hops)]
            comes.append(lax.ppermute(block, "hop", route))
        else:
            stays.append(block)


def small_call(kernel, *arrays, out):
    vmem = pl.BlockSpec(memory_space=pltpu.VMEM)
    return pl.pallas_call(
        kernel,
        in_specs=[vmem] * len(arrays),
        out_specs=jax.tree.map(lambda _: vmem, out),
        out_shape=out,
        compiler_params=pltpu.CompilerParams(vmem_limit_bytes=16 << 20),
    )(*arrays)


def wide(shape):
    return jax.ShapeDtypeStruct(shape, jnp.float32)


def thin(shape):
    return jax.ShapeDtypeStruct(shape, jnp.bfloat16)


def by_side_kernel(kept, taken, stay, leave):
    side = lax.axis_index("side")
    leave[...] = (kept[:, 1 - side] + taken[:, 1 - side].astype(jnp.float32)).astype(leave.dtype)
    stay[...] = kept[:, side] + taken[:, side].astype(jnp.float32)


def by_side(kept, taken):
    count, _, rows, half = kept.shape
    shape = (count, rows, half)
    return small_call(by_side_kernel, kept, taken, out=(wide(shape), thin(shape)))


def by_hop_kernel(kept, taken, *outs):
    for index, out in enumerate(outs):
        out[...] = (kept[index] + taken[index].astype(jnp.float32)).astype(out.dtype)


def line_kernel(steps, kept, taken, out):
    place, hops = lax.axis_index("hop"), lax.axis_size("hop")
    for index, step in enumerate(steps):
        total = kept[index] + taken[index].astype(jnp.float32)
        out[(place + step) % hops] = total.astype(out.dtype)


def add_kernel(first, *refs):
    *others, out = refs
    total = first[...].astype(jnp.float32)
    for other in others:
        total = total + other[...].astype(jnp.float32)
    out[...] = total.astype(out.dtype)


def over_clip(mine, swap):
    sets = lax.axis_size("set")
    if sets == 2:
        terms = (mine, lax.ppermute(mine, "set", swap))
    else:
        terms = tuple(lax.all_gather(mine, "set", axis=0, tiled=False))
    total = small_call(add_kernel, *terms, out=wide(mine.shape))
    return total, lax.ppermute(total, "core", swap)


def update_kernel(shift, part, *refs):
    state, outs, news, sems = refs[:3], refs[-9:-6], refs[-6:-3], refs[-3:]
    half = part.shape[1]
    side = (lax.axis_index("core") + shift) % 2
    columns = pl.ds(pl.multiple_of(side * half, 128), half)
    copies = []
    for out, new, sem, value in zip(
        outs, news, sems, adamw(*(ref[:, columns] for ref in state), part[...])
    ):
        new[...] = value
        copies.append(pltpu.make_async_copy(new, out.at[:, columns], sem))
        copies[-1].start()
    for copy in copies:
        copy.wait()


def update_columns(whose, part, state, outs=()):
    vmem, anywhere = (pl.BlockSpec(memory_space=space) for space in (pltpu.VMEM, pl.ANY))
    return pl.pallas_call(
        functools.partial(update_kernel, int(whose == "other")),
        in_specs=[vmem] * (1 + len(state)) + [anywhere] * len(outs),
        out_specs=(anywhere,) * 3,
        out_shape=(wide(state[0].shape),) * 3,
        scratch_shapes=[pltpu.VMEM(part.shape, part.dtype)] * 3 + [pltpu.SemaphoreType.DMA] * 3,
        input_output_aliases={1 + len(state) + i: i for i in range(len(outs))},
        compiler_params=pltpu.CompilerParams(vmem_limit_bytes=16 << 20),
    )(part, *state, *outs)


STREAM = ("one", "two", "three", "four", "five", "six")


def solution(mesh):
    clip, frames = mesh.shape["clip"], mesh.shape["tm"]
    grid = Mesh(
        mesh.devices.reshape(clip // 2, 2, frames // 2, 2), ("set", "core", "hop", "side")
    )
    seq, tok = ("set", "core"), ("hop", "side")
    wide = P(seq, tok, None)
    rows = P(tok, None)
    in_specs = (wide,) * 5 + (P(seq, None),) + (rows,) * 3

    return jax.shard_map(body, mesh=grid, in_specs=in_specs, out_specs=(rows,) * 3, check_vma=False)
```

profile of v0, /device:TPU:0, one launch (start us, length us, event | category | flops | bytes accessed | tf_op | source)
XLA Modules:
  0.0 88.1 jit_solution(3048736998370952380)
XLA Ops:
  0.6 1.3 %cut_out.2 = (bf16[176,768]{1,0:T(8,128)(2,1)S(1)}, bf16[144,768]{1,0:T(8,128)(2,1)S(1)}, bf16[176,768]{1,0:T(8,128)(2,1)S(1)}, bf16[144,768]{1,0:T(8,128)(2,1)S(1)}, bf16[176,768]{1,0:T(8,128)(2,1)S(1)}) custom-call(bf16[320,768]{1,0:T(8,128)(2,1)} %bitcast.5, bf16[320,768]{1,0:T(8,128)(2,1)} %bitcast.14, bf16[320,768]{1,0:T(8,128)(2,1)} %bitcast.10), custom_call_target="tpu_custom_call" | custom-call | tf_op jit(solution)/shard_map/cut_out/pallas_call | solution.py:66
  2.0 5.0 %collective-permute-start.1 = (bf16[176,768]{1,0:T(8,128)(2,1)S(1)}, bf16[176,768]{1,0:T(8,128)(2,1)S(1)}, u32[]{:S(2)}, u32[]{:S(2)}) collective-permute-start(bf16[176,768]{1,0:T(8,128)(2,1)S(1)} %get-tuple-element.22), channel_id=1, source_target_pairs={{0,2},{1,3},{2,4},{3,5},{4,6},{5,7},{8,10},{9,11},{10,12},{11,13},... | collective-permute-start | bytes 811016 | tf_op jit(solution)/shard_map/ppermute | solution.py:305
  7.0 3.5 %collective-permute-start = (bf16[144,768]{1,0:T(8,128)(2,1)S(1)}, bf16[144,768]{1,0:T(8,128)(2,1)S(1)}, u32[]{:S(2)}, u32[]{:S(2)}) collective-permute-start(bf16[144,768]{1,0:T(8,128)(2,1)S(1)} %get-tuple-element.21), channel_id=1, source_target_pairs={{0,2},{1,3},{2,4},{3,5},{4,6},{5,7},{8,10},{9,11},{10,12},{11,13},... | collective-permute-start | bytes 663560 | tf_op jit(solution)/shard_map/ppermute | solution.py:305
  10.4 3.5 %collective-permute-start.5 = (bf16[176,768]{1,0:T(8,128)(2,1)S(1)}, bf16[176,768]{1,0:T(8,128)(2,1)S(1)}, u32[]{:S(2)}, u32[]{:S(2)}) collective-permute-start(bf16[176,768]{1,0:T(8,128)(2,1)S(1)} %get-tuple-element.23), channel_id=1, source_target_pairs={{0,2},{1,3},{2,4},{3,5},{4,6},{5,7},{8,10},{9,11},{10,12},{11,13},... | collective-permute-start | bytes 811016 | tf_op jit(solution)/shard_map/ppermute | solution.py:305
  13.9 1.9 %collective-permute-start.9 = (bf16[176,768]{1,0:T(8,128)(2,1)S(1)}, bf16[176,768]{1,0:T(8,128)(2,1)S(1)}, u32[]{:S(2)}, u32[]{:S(2)}) collective-permute-start(bf16[176,768]{1,0:T(8,128)(2,1)S(1)} %get-tuple-element.25), channel_id=1, source_target_pairs={{0,2},{1,3},{2,4},{3,5},{4,6},{5,7},{8,10},{9,11},{10,12},{11,13},... | collective-permute-start | bytes 811016 | tf_op jit(solution)/shard_map/ppermute | solution.py:305
  15.9 1.9 %collective-permute-start.8 = (bf16[144,768]{1,0:T(8,128)(2,1)S(1)}, bf16[144,768]{1,0:T(8,128)(2,1)S(1)}, u32[]{:S(2)}, u32[]{:S(2)}) collective-permute-start(bf16[144,768]{1,0:T(8,128)(2,1)S(1)} %get-tuple-element.24), channel_id=1, source_target_pairs={{0,2},{1,3},{2,4},{3,5},{4,6},{5,7},{8,10},{9,11},{10,12},{11,13},... | collective-permute-start | bytes 663560 | tf_op jit(solution)/shard_map/ppermute | solution.py:305
  17.8 0.9 %cut_out.3 = bf16[144,768]{1,0:T(8,128)(2,1)S(1)} custom-call(bf16[320,768]{1,0:T(8,128)(2,1)} %bitcast.6), custom_call_target="tpu_custom_call" | custom-call | tf_op jit(solution)/shard_map/cut_out/pallas_call | solution.py:66
  18.8 4.2 %collective-permute-start.4 = (bf16[144,768]{1,0:T(8,128)(2,1)S(1)}, bf16[144,768]{1,0:T(8,128)(2,1)S(1)}, u32[]{:S(2)}, u32[]{:S(2)}) collective-permute-start(bf16[144,768]{1,0:T(8,128)(2,1)S(1)} %cut_out.3), channel_id=1, source_target_pairs={{0,2},{1,3},{2,4},{3,5},{4,6},{5,7},{8,10},{9,11},{10,12},{11,13},... | collective-permute-start | bytes 663560 | tf_op jit(solution)/shard_map/ppermute | solution.py:305
  22.9 1.0 %picked.6 = bf16[144,768]{1,0:T(8,128)(2,1)S(1)} custom-call(bf16[144,768]{1,0:T(8,128)(2,1)S(1)} %collective-permute-done.refs_1_.far, bf16[320,768]{1,0:T(8,128)(2,1)} %bitcast.11), custom_call_target="tpu_custom_call" | custom-call | tf_op jit(solution)/shard_map/picked/pallas_call | solution.py:95
  23.9 0.9 %collective-permute-start.2 = (bf16[144,768]{1,0:T(8,128)(2,1)S(1)}, bf16[144,768]{1,0:T(8,128)(2,1)S(1)}, u32[]{:S(2)}, u32[]{:S(2)}) collective-permute-start(bf16[144,768]{1,0:T(8,128)(2,1)S(1)} %picked.6), channel_id=1, source_target_pairs={{0,1},{1,0},{2,3},{3,2},{4,5},{5,4},{6,7},{7,6},{8,9},{9,8},{10,11... | collective-permute-start | bytes 663560 | tf_op jit(solution)/shard_map/ppermute | solution.py:307
  24.8 1.0 %picked.7 = bf16[176,768]{1,0:T(8,128)(2,1)S(1)} custom-call(bf16[176,768]{1,0:T(8,128)(2,1)S(1)} %collective-permute-done.1.refs_2_.far, bf16[320,768]{1,0:T(8,128)(2,1)} %bitcast.12), custom_call_target="tpu_custom_call" | custom-call | tf_op jit(solution)/shard_map/picked/pallas_call | solution.py:95
  26.1 1.0 %picked.9 = bf16[176,768]{1,0:T(8,128)(2,1)S(1)} custom-call(bf16[176,768]{1,0:T(8,128)(2,1)S(1)} %collective-permute-done.5.far.refs_2_, bf16[320,768]{1,0:T(8,128)(2,1)} %bitcast.7), custom_call_target="tpu_custom_call" | custom-call | tf_op jit(solution)/shard_map/picked/pallas_call | solution.py:95
  27.1 3.0 %collective-permute-done.9.far.refs_7_ = bf16[176,768]{1,0:T(8,128)(2,1)S(1)} collective-permute-done((bf16[176,768]{1,0:T(8,128)(2,1)S(1)}, bf16[176,768]{1,0:T(8,128)(2,1)S(1)}, u32[]{:S(2)}, u32[]{:S(2)}) %collective-permute-start.9) | collective-permute-done | bytes 270368 | tf_op jit(solution)/shard_map/ppermute | solution.py:305
  30.1 1.5 %collective-permute-start.7 = (bf16[176,768]{1,0:T(8,128)(2,1)S(1)}, bf16[176,768]{1,0:T(8,128)(2,1)S(1)}, u32[]{:S(2)}, u32[]{:S(2)}) collective-permute-start(bf16[176,768]{1,0:T(8,128)(2,1)S(1)} %picked.9), channel_id=1, source_target_pairs={{0,1},{1,0},{2,3},{3,2},{4,5},{5,4},{6,7},{7,6},{8,9},{9,8},{10,11... | collective-permute-start | bytes 811016 | tf_op jit(solution)/shard_map/ppermute | solution.py:307
  31.6 1.0 %picked.11 = bf16[176,768]{1,0:T(8,128)(2,1)S(1)} custom-call(bf16[176,768]{1,0:T(8,128)(2,1)S(1)} %collective-permute-done.9.far.refs_7_, bf16[320,768]{1,0:T(8,128)(2,1)} %bitcast.15), custom_call_target="tpu_custom_call" | custom-call | tf_op jit(solution)/shard_map/picked/pallas_call | solution.py:95
  32.6 2.3 %collective-permute-done.8.far.refs_6_ = bf16[144,768]{1,0:T(8,128)(2,1)S(1)} collective-permute-done((bf16[144,768]{1,0:T(8,128)(2,1)S(1)}, bf16[144,768]{1,0:T(8,128)(2,1)S(1)}, u32[]{:S(2)}, u32[]{:S(2)}) %collective-permute-start.8) | collective-permute-done | bytes 221216 | tf_op jit(solution)/shard_map/ppermute | solution.py:305
  34.9 1.5 %collective-permute-start.11 = (bf16[176,768]{1,0:T(8,128)(2,1)S(1)}, bf16[176,768]{1,0:T(8,128)(2,1)S(1)}, u32[]{:S(2)}, u32[]{:S(2)}) collective-permute-start(bf16[176,768]{1,0:T(8,128)(2,1)S(1)} %picked.11), channel_id=1, source_target_pairs={{0,1},{1,0},{2,3},{3,2},{4,5},{5,4},{6,7},{7,6},{8,9},{9,8},{10,11... | collective-permute-start | bytes 811016 | tf_op jit(solution)/shard_map/ppermute | solution.py:307
  36.4 0.9 %picked.10 = bf16[144,768]{1,0:T(8,128)(2,1)S(1)} custom-call(bf16[144,768]{1,0:T(8,128)(2,1)S(1)} %collective-permute-done.8.far.refs_6_, bf16[320,768]{1,0:T(8,128)(2,1)} %bitcast.16), custom_call_target="tpu_custom_call" | custom-call | tf_op jit(solution)/shard_map/picked/pallas_call | solution.py:95
  37.3 1.1 %collective-permute-done.4.far.refs_1_ = bf16[144,768]{1,0:T(8,128)(2,1)S(1)} collective-permute-done((bf16[144,768]{1,0:T(8,128)(2,1)S(1)}, bf16[144,768]{1,0:T(8,128)(2,1)S(1)}, u32[]{:S(2)}, u32[]{:S(2)}) %collective-permute-start.4) | collective-permute-done | bytes 221216 | tf_op jit(solution)/shard_map/ppermute | solution.py:305
  38.5 1.5 %collective-permute-start.10 = (bf16[144,768]{1,0:T(8,128)(2,1)S(1)}, bf16[144,768]{1,0:T(8,128)(2,1)S(1)}, u32[]{:S(2)}, u32[]{:S(2)}) collective-permute-start(bf16[144,768]{1,0:T(8,128)(2,1)S(1)} %picked.10), channel_id=1, source_target_pairs={{0,1},{1,0},{2,3},{3,2},{4,5},{5,4},{6,7},{7,6},{8,9},{9,8},{10,11... | collective-permute-start | bytes 663560 | tf_op jit(solution)/shard_map/ppermute | solution.py:307
  40.0 0.9 %picked.8 = bf16[144,768]{1,0:T(8,128)(2,1)S(1)} custom-call(bf16[144,768]{1,0:T(8,128)(2,1)S(1)} %collective-permute-done.4.far.refs_1_, bf16[320,768]{1,0:T(8,128)(2,1)} %bitcast.8), custom_call_target="tpu_custom_call" | custom-call | tf_op jit(solution)/shard_map/picked/pallas_call | solution.py:95
  41.6 11.7 %collective-permute-done.10.refs_8_ = bf16[144,768]{1,0:T(8,128)(2,1)S(1)} collective-permute-done((bf16[144,768]{1,0:T(8,128)(2,1)S(1)}, bf16[144,768]{1,0:T(8,128)(2,1)S(1)}, u32[]{:S(2)}, u32[]{:S(2)}) %collective-permute-start.10) | collective-permute-done | bytes 221216 | tf_op jit(solution)/shard_map/ppermute | solution.py:307
  53.4 2.4 %collective-permute-done.6.refs_3_ = bf16[144,768]{1,0:T(8,128)(2,1)S(1)} collective-permute-done((bf16[144,768]{1,0:T(8,128)(2,1)S(1)}, bf16[144,768]{1,0:T(8,128)(2,1)S(1)}, u32[]{:S(2)}, u32[]{:S(2)}) %collective-permute-start.6) | collective-permute-done | bytes 221216 | tf_op jit(solution)/shard_map/ppermute | solution.py:307
  55.8 6.9 %key_grads.1.parts = bf16[960,768]{1,0:T(8,128)(2,1)S(1)} custom-call(s32[1,8]{1,0:T(1,128)S(1)} %copy-done.8, bf16[320,768]{1,0:T(8,128)(2,1)S(1)} %bitcast.18, bf16[320,768]{1,0:T(8,128)(2,1)S(1)} %bitcast.19, bf16[320,768]{1,0:T(8,128)(2,1)S(1)} %bitcast.9, bf16[144,768]{1,0:T(8,128)(2,1)S(1)} %collective-permute-done.4.far.refs_1_, ...), custom_call_target="tpu_custom_call" | custom-call | tf_op jit(solution)/shard_map/key_grads/pallas_call | solution.py:203
  65.5 0.9 %collective-permute-start.15 = (bf16[2,96,384]{2,1,0:T(8,128)(2,1)S(1)}, bf16[2,96,384]{2,1,0:T(8,128)(2,1)S(1)}, u32[]{:S(2)}, u32[]{:S(2)}) collective-permute-start(bf16[2,96,384]{2,1,0:T(8,128)(2,1)S(1)} %get-tuple-element.32), channel_id=1, source_target_pairs={{0,1},{1,0},{2,3},{3,2},{4,5},{5,4},{6,7},{7,6},{8,9},{9,8},{10,11... | collective-permute-start | bytes 442376 | tf_op jit(solution)/shard_map/ppermute | solution.py:333
  66.5 1.2 %collective-permute-start.13 = (bf16[2,96,384]{2,1,0:T(8,128)(2,1)S(1)}, bf16[2,96,384]{2,1,0:T(8,128)(2,1)S(1)}, u32[]{:S(2)}, u32[]{:S(2)}) collective-permute-start(bf16[2,96,384]{2,1,0:T(8,128)(2,1)S(1)} %get-tuple-element.29), channel_id=1, source_target_pairs={{0,1},{1,0},{2,3},{3,2},{4,5},{5,4},{6,7},{7,6},{8,9},{9,8},{10,11... | collective-permute-start | bytes 442376 | tf_op jit(solution)/shard_map/ppermute | solution.py:333
  67.8 4.6 %collective-permute-done.15.taken = bf16[2,96,384]{2,1,0:T(8,128)(2,1)S(1)} collective-permute-done((bf16[2,96,384]{2,1,0:T(8,128)(2,1)S(1)}, bf16[2,96,384]{2,1,0:T(8,128)(2,1)S(1)}, u32[]{:S(2)}, u32[]{:S(2)}) %collective-permute-start.15) | collective-permute-done | bytes 147488 | tf_op jit(solution)/shard_map/ppermute | solution.py:333
  72.4 2.6 %collective-permute-start.16 = (bf16[96,384]{1,0:T(8,128)(2,1)S(1)}, bf16[96,384]{1,0:T(8,128)(2,1)S(1)}, u32[]{:S(2)}, u32[]{:S(2)}) collective-permute-start(bf16[96,384]{1,0:T(8,128)(2,1)S(1)} %get-tuple-element.33), channel_id=1, source_target_pairs={{0,4},{2,6},{4,0},{6,2},{1,5},{3,7},{5,1},{7,3},{8,12},{10,14},{12... | collective-permute-start | bytes 221192 | tf_op jit(solution)/shard_map/ppermute | solution.py:362
  75.5 3.5 %collective-permute-start.18 = (bf16[96,384]{1,0:T(8,128)(2,1)S(1)}, bf16[96,384]{1,0:T(8,128)(2,1)S(1)}, u32[]{:S(2)}, u32[]{:S(2)}) collective-permute-start(bf16[96,384]{1,0:T(8,128)(2,1)S(1)} %get-tuple-element.35), channel_id=1, source_target_pairs={{0,6},{2,0},{4,2},{6,4},{1,7},{3,1},{5,3},{7,5},{8,14},{10,8},{12,... | collective-permute-start | bytes 221192 | tf_op jit(solution)/shard_map/ppermute | solution.py:362
  79.6 1.7 %collective-permute-done.17.refs_1_ = bf16[96,384]{1,0:T(8,128)(2,1)S(1)} collective-permute-done((bf16[96,384]{1,0:T(8,128)(2,1)S(1)}, bf16[96,384]{1,0:T(8,128)(2,1)S(1)}, u32[]{:S(2)}, u32[]{:S(2)}) %collective-permute-start.17) | collective-permute-done | bytes 73760 | tf_op jit(solution)/shard_map/ppermute | solution.py:362
  81.3 1.6 %collective-permute-start.19 = (bf16[96,384]{1,0:T(8,128)(2,1)S(1)}, bf16[96,384]{1,0:T(8,128)(2,1)S(1)}, u32[]{:S(2)}, u32[]{:S(2)}) collective-permute-start(bf16[96,384]{1,0:T(8,128)(2,1)S(1)} %shard_map.116.first), channel_id=1, source_target_pairs={{0,16},{16,0},{1,17},{17,1},{2,18},{18,2},{3,19},{19,3},{4,20},{20... | collective-permute-start | bytes 221192 | tf_op jit(solution)/shard_map/ppermute | solution.py:421
  82.9 2.9 %collective-permute-done.19.refs_0_ = bf16[96,384]{1,0:T(8,128)(2,1)S(1)} collective-permute-done((bf16[96,384]{1,0:T(8,128)(2,1)S(1)}, bf16[96,384]{1,0:T(8,128)(2,1)S(1)}, u32[]{:S(2)}, u32[]{:S(2)}) %collective-permute-start.19) | collective-permute-done | bytes 73760 | tf_op jit(solution)/shard_map/ppermute | solution.py:421
  (50 shorter events, 7.3 us)
Async XLA Ops:
  2.0 21.9 %collective-permute-start.1 = (bf16[176,768]{1,0:T(8,128)(2,1)S(1)}, bf16[176,768]{1,0:T(8,128)(2,1)S(1)}, u32[]{:S(2)}, u32[]{:S(2)}) collective-permute-start(bf16[176,768]{1,0:T(8,128)(2,1)S(1)} %get-tuple-element.22), channel_id=1, source_target_pairs={{0,2},{1,3},{2,4},{3,5},{4,6},{5,7},{8,10},{9,11},{10,12},{11,13},... | collective-permute-start | bytes 811016 | tf_op jit(solution)/shard_map/ppermute | solution.py:305
  7.0 11.8 %collective-permute-start = (bf16[144,768]{1,0:T(8,128)(2,1)S(1)}, bf16[144,768]{1,0:T(8,128)(2,1)S(1)}, u32[]{:S(2)}, u32[]{:S(2)}) collective-permute-start(bf16[144,768]{1,0:T(8,128)(2,1)S(1)} %get-tuple-element.21), channel_id=1, source_target_pairs={{0,2},{1,3},{2,4},{3,5},{4,6},{5,7},{8,10},{9,11},{10,12},{11,13},... | collective-permute-start | bytes 663560 | tf_op jit(solution)/shard_map/ppermute | solution.py:305
  10.4 15.4 %collective-permute-start.5 = (bf16[176,768]{1,0:T(8,128)(2,1)S(1)}, bf16[176,768]{1,0:T(8,128)(2,1)S(1)}, u32[]{:S(2)}, u32[]{:S(2)}) collective-permute-start(bf16[176,768]{1,0:T(8,128)(2,1)S(1)} %get-tuple-element.23), channel_id=1, source_target_pairs={{0,2},{1,3},{2,4},{3,5},{4,6},{5,7},{8,10},{9,11},{10,12},{11,13},... | collective-permute-start | bytes 811016 | tf_op jit(solution)/shard_map/ppermute | solution.py:305
  13.9 16.2 %collective-permute-start.9 = (bf16[176,768]{1,0:T(8,128)(2,1)S(1)}, bf16[176,768]{1,0:T(8,128)(2,1)S(1)}, u32[]{:S(2)}, u32[]{:S(2)}) collective-permute-start(bf16[176,768]{1,0:T(8,128)(2,1)S(1)} %get-tuple-element.25), channel_id=1, source_target_pairs={{0,2},{1,3},{2,4},{3,5},{4,6},{5,7},{8,10},{9,11},{10,12},{11,13},... | collective-permute-start | bytes 811016 | tf_op jit(solution)/shard_map/ppermute | solution.py:305
  15.9 19.0 %collective-permute-start.8 = (bf16[144,768]{1,0:T(8,128)(2,1)S(1)}, bf16[144,768]{1,0:T(8,128)(2,1)S(1)}, u32[]{:S(2)}, u32[]{:S(2)}) collective-permute-start(bf16[144,768]{1,0:T(8,128)(2,1)S(1)} %get-tuple-element.24), channel_id=1, source_target_pairs={{0,2},{1,3},{2,4},{3,5},{4,6},{5,7},{8,10},{9,11},{10,12},{11,13},... | collective-permute-start | bytes 663560 | tf_op jit(solution)/shard_map/ppermute | solution.py:305
  18.8 19.7 %collective-permute-start.4 = (bf16[144,768]{1,0:T(8,128)(2,1)S(1)}, bf16[144,768]{1,0:T(8,128)(2,1)S(1)}, u32[]{:S(2)}, u32[]{:S(2)}) collective-permute-start(bf16[144,768]{1,0:T(8,128)(2,1)S(1)} %cut_out.3), channel_id=1, source_target_pairs={{0,2},{1,3},{2,4},{3,5},{4,6},{5,7},{8,10},{9,11},{10,12},{11,13},... | collective-permute-start | bytes 663560 | tf_op jit(solution)/shard_map/ppermute | solution.py:305
  23.9 17.1 %collective-permute-start.2 = (bf16[144,768]{1,0:T(8,128)(2,1)S(1)}, bf16[144,768]{1,0:T(8,128)(2,1)S(1)}, u32[]{:S(2)}, u32[]{:S(2)}) collective-permute-start(bf16[144,768]{1,0:T(8,128)(2,1)S(1)} %picked.6), channel_id=1, source_target_pairs={{0,1},{1,0},{2,3},{3,2},{4,5},{5,4},{6,7},{7,6},{8,9},{9,8},{10,11... | collective-permute-start | bytes 663560 | tf_op jit(solution)/shard_map/ppermute | solution.py:307
  25.8 15.6 %collective-permute-start.3 = (bf16[176,768]{1,0:T(8,128)(2,1)S(1)}, bf16[176,768]{1,0:T(8,128)(2,1)S(1)}, u32[]{:S(2)}, u32[]{:S(2)}) collective-permute-start(bf16[176,768]{1,0:T(8,128)(2,1)S(1)} %picked.7), channel_id=1, source_target_pairs={{0,1},{1,0},{2,3},{3,2},{4,5},{5,4},{6,7},{7,6},{8,9},{9,8},{10,11... | collective-permute-start | bytes 811016 | tf_op jit(solution)/shard_map/ppermute | solution.py:307
  27.1 14.0 %copy-start.1 = (bf16[1,320,768]{2,1,0:T(8,128)(2,1)S(1)}, bf16[1,320,768]{2,1,0:T(8,128)(2,1)}, u32[]{:S(2)}) copy-start(bf16[1,320,768]{2,1,0:T(8,128)(2,1)} %param.9) | copy-start | bytes 1474564
  30.1 25.6 %collective-permute-start.7 = (bf16[176,768]{1,0:T(8,128)(2,1)S(1)}, bf16[176,768]{1,0:T(8,128)(2,1)S(1)}, u32[]{:S(2)}, u32[]{:S(2)}) collective-permute-start(bf16[176,768]{1,0:T(8,128)(2,1)S(1)} %picked.9), channel_id=1, source_target_pairs={{0,1},{1,0},{2,3},{3,2},{4,5},{5,4},{6,7},{7,6},{8,9},{9,8},{10,11... | collective-permute-start | bytes 811016 | tf_op jit(solution)/shard_map/ppermute | solution.py:307
  34.9 20.9 %collective-permute-start.11 = (bf16[176,768]{1,0:T(8,128)(2,1)S(1)}, bf16[176,768]{1,0:T(8,128)(2,1)S(1)}, u32[]{:S(2)}, u32[]{:S(2)}) collective-permute-start(bf16[176,768]{1,0:T(8,128)(2,1)S(1)} %picked.11), channel_id=1, source_target_pairs={{0,1},{1,0},{2,3},{3,2},{4,5},{5,4},{6,7},{7,6},{8,9},{9,8},{10,11... | collective-permute-start | bytes 811016 | tf_op jit(solution)/shard_map/ppermute | solution.py:307
  38.5 14.9 %collective-permute-start.10 = (bf16[144,768]{1,0:T(8,128)(2,1)S(1)}, bf16[144,768]{1,0:T(8,128)(2,1)S(1)}, u32[]{:S(2)}, u32[]{:S(2)}) collective-permute-start(bf16[144,768]{1,0:T(8,128)(2,1)S(1)} %picked.10), channel_id=1, source_target_pairs={{0,1},{1,0},{2,3},{3,2},{4,5},{5,4},{6,7},{7,6},{8,9},{9,8},{10,11... | collective-permute-start | bytes 663560 | tf_op jit(solution)/shard_map/ppermute | solution.py:307
  40.9 14.8 %copy-start = (bf16[1,320,768]{2,1,0:T(8,128)(2,1)S(1)}, bf16[1,320,768]{2,1,0:T(8,128)(2,1)}, u32[]{:S(2)}) copy-start(bf16[1,320,768]{2,1,0:T(8,128)(2,1)} %param.11) | copy-start | bytes 1474564
  41.0 14.8 %copy-start.2 = (bf16[1,320,768]{2,1,0:T(8,128)(2,1)S(1)}, bf16[1,320,768]{2,1,0:T(8,128)(2,1)}, u32[]{:S(2)}) copy-start(bf16[1,320,768]{2,1,0:T(8,128)(2,1)} %param.12) | copy-start | bytes 1474564
  41.0 14.8 %copy-start.6 = (bf16[1,320,768]{2,1,0:T(8,128)(2,1)S(1)}, bf16[1,320,768]{2,1,0:T(8,128)(2,1)}, u32[]{:S(2)}) copy-start(bf16[1,320,768]{2,1,0:T(8,128)(2,1)} %param.10) | copy-start | bytes 1474564
  41.0 14.8 %copy-start.7 = (bf16[1,320,768]{2,1,0:T(8,128)(2,1)S(1)}, bf16[1,320,768]{2,1,0:T(8,128)(2,1)}, u32[]{:S(2)}) copy-start(bf16[1,320,768]{2,1,0:T(8,128)(2,1)} %param.13) | copy-start | bytes 1474564
  41.0 14.8 %copy-start.8 = (s32[1,8]{1,0:T(1,128)S(1)}, s32[1,8]{1,0:T(1,128)}, u32[]{:S(2)}) copy-start(s32[1,8]{1,0:T(1,128)} %flags.1) | copy-start | bytes 100
  41.0 14.7 %collective-permute-start.6 = (bf16[144,768]{1,0:T(8,128)(2,1)S(1)}, bf16[144,768]{1,0:T(8,128)(2,1)S(1)}, u32[]{:S(2)}, u32[]{:S(2)}) collective-permute-start(bf16[144,768]{1,0:T(8,128)(2,1)S(1)} %picked.8), channel_id=1, source_target_pairs={{0,1},{1,0},{2,3},{3,2},{4,5},{5,4},{6,7},{7,6},{8,9},{9,8},{10,11... | collective-permute-start | bytes 663560 | tf_op jit(solution)/shard_map/ppermute | solution.py:307
  63.3 2.2 %collective-permute-start.14 = (bf16[2,2,96,384]{3,2,1,0:T(8,128)(2,1)S(1)}, bf16[2,2,96,384]{3,2,1,0:T(8,128)(2,1)S(1)}, u32[]{:S(2)}, u32[]{:S(2)}) collective-permute-start(bf16[2,2,96,384]{3,2,1,0:T(8,128)(2,1)S(1)} %partial_gradient.5), channel_id=1, source_target_pairs={{0,8},{8,0},{1,9},{9,1},{2,10},{10,2},{3,11},{11,3},{4,12},{12,4},... | collective-permute-start | bytes 884744 | tf_op jit(solution)/shard_map/ppermute | solution.py:331
  64.2 2.2 %collective-permute-start.12 = (bf16[2,2,96,384]{3,2,1,0:T(8,128)(2,1)S(1)}, bf16[2,2,96,384]{3,2,1,0:T(8,128)(2,1)S(1)}, u32[]{:S(2)}, u32[]{:S(2)}) collective-permute-start(bf16[2,2,96,384]{3,2,1,0:T(8,128)(2,1)S(1)} %get-tuple-element.27), channel_id=1, source_target_pairs={{0,8},{8,0},{1,9},{9,1},{2,10},{10,2},{3,11},{11,3},{4,12},{12,4},... | collective-permute-start | bytes 884744 | tf_op jit(solution)/shard_map/ppermute | solution.py:331
  65.5 20.3 %copy-start.3 = (f32[96,768]{1,0:T(8,128)S(1)}, f32[96,768]{1,0:T(8,128)}, u32[]{:S(2)}) copy-start(f32[96,768]{1,0:T(8,128)} %refs_0_.3) | copy-start | bytes 884740
  65.5 20.3 %copy-start.4 = (f32[96,768]{1,0:T(8,128)S(1)}, f32[96,768]{1,0:T(8,128)}, u32[]{:S(2)}) copy-start(f32[96,768]{1,0:T(8,128)} %refs_1_.3) | copy-start | bytes 884740
  65.5 20.3 %copy-start.5 = (f32[96,768]{1,0:T(8,128)S(1)}, f32[96,768]{1,0:T(8,128)}, u32[]{:S(2)}) copy-start(f32[96,768]{1,0:T(8,128)} %refs_2_.3) | copy-start | bytes 884740
  65.5 6.8 %collective-permute-start.15 = (bf16[2,96,384]{2,1,0:T(8,128)(2,1)S(1)}, bf16[2,96,384]{2,1,0:T(8,128)(2,1)S(1)}, u32[]{:S(2)}, u32[]{:S(2)}) collective-permute-start(bf16[2,96,384]{2,1,0:T(8,128)(2,1)S(1)} %get-tuple-element.32), channel_id=1, source_target_pairs={{0,1},{1,0},{2,3},{3,2},{4,5},{5,4},{6,7},{7,6},{8,9},{9,8},{10,11... | collective-permute-start | bytes 442376 | tf_op jit(solution)/shard_map/ppermute | solution.py:333
  66.5 8.9 %collective-permute-start.13 = (bf16[2,96,384]{2,1,0:T(8,128)(2,1)S(1)}, bf16[2,96,384]{2,1,0:T(8,128)(2,1)S(1)}, u32[]{:S(2)}, u32[]{:S(2)}) collective-permute-start(bf16[2,96,384]{2,1,0:T(8,128)(2,1)S(1)} %get-tuple-element.29), channel_id=1, source_target_pairs={{0,1},{1,0},{2,3},{3,2},{4,5},{5,4},{6,7},{7,6},{8,9},{9,8},{10,11... | collective-permute-start | bytes 442376 | tf_op jit(solution)/shard_map/ppermute | solution.py:333
  72.4 7.2 %collective-permute-start.16 = (bf16[96,384]{1,0:T(8,128)(2,1)S(1)}, bf16[96,384]{1,0:T(8,128)(2,1)S(1)}, u32[]{:S(2)}, u32[]{:S(2)}) collective-permute-start(bf16[96,384]{1,0:T(8,128)(2,1)S(1)} %get-tuple-element.33), channel_id=1, source_target_pairs={{0,4},{2,6},{4,0},{6,2},{1,5},{3,7},{5,1},{7,3},{8,12},{10,14},{12... | collective-permute-start | bytes 221192 | tf_op jit(solution)/shard_map/ppermute | solution.py:362
  75.0 6.3 %collective-permute-start.17 = (bf16[96,384]{1,0:T(8,128)(2,1)S(1)}, bf16[96,384]{1,0:T(8,128)(2,1)S(1)}, u32[]{:S(2)}, u32[]{:S(2)}) collective-permute-start(bf16[96,384]{1,0:T(8,128)(2,1)S(1)} %get-tuple-element.34), channel_id=1, source_target_pairs={{0,2},{2,4},{4,6},{6,0},{1,3},{3,5},{5,7},{7,1},{8,10},{10,12},{12... | collective-permute-start | bytes 221192 | tf_op jit(solution)/shard_map/ppermute | solution.py:362
  75.5 5.8 %collective-permute-start.18 = (bf16[96,384]{1,0:T(8,128)(2,1)S(1)}, bf16[96,384]{1,0:T(8,128)(2,1)S(1)}, u32[]{:S(2)}, u32[]{:S(2)}) collective-permute-start(bf16[96,384]{1,0:T(8,128)(2,1)S(1)} %get-tuple-element.35), channel_id=1, source_target_pairs={{0,6},{2,0},{4,2},{6,4},{1,7},{3,1},{5,3},{7,5},{8,14},{10,8},{12,... | collective-permute-start | bytes 221192 | tf_op jit(solution)/shard_map/ppermute | solution.py:362
  81.3 4.4 %collective-permute-start.19 = (bf16[96,384]{1,0:T(8,128)(2,1)S(1)}, bf16[96,384]{1,0:T(8,128)(2,1)S(1)}, u32[]{:S(2)}, u32[]{:S(2)}) collective-permute-start(bf16[96,384]{1,0:T(8,128)(2,1)S(1)} %shard_map.116.first), channel_id=1, source_target_pairs={{0,16},{16,0},{1,17},{17,1},{2,18},{18,2},{3,19},{19,3},{4,20},{20... | collective-permute-start | bytes 221192 | tf_op jit(solution)/shard_map/ppermute | solution.py:421
  85.8 1.4 %collective-permute-start.20 = (f32[96,384]{1,0:T(8,128)S(1)}, f32[96,384]{1,0:T(8,128)S(1)}, u32[]{:S(2)}, u32[]{:S(2)}) collective-permute-start(f32[96,384]{1,0:T(8,128)S(1)} %shard_map.117.part), channel_id=1, source_target_pairs={{0,8},{8,0},{1,9},{9,1},{2,10},{10,2},{3,11},{11,3},{4,12},{12,4},... | collective-permute-start | bytes 442376 | tf_op jit(solution)/shard_map/ppermute | solution.py:425
where the time goes:
time: 88.6 us; the launch traced here: 88.1 us
  starting transfers between devices  36.8 us (42%)
  waiting for transfers between devices  30.7 us (35%)
  Pallas kernels  19.5 us (22%)
  between operations  1.03 us (1%)
    ppermute x6, starting transfers between devices, behind(): lax.ppermute(value, ('hop', 'side'), [(i, i + 2) for i in range(frames -...  19.9 us
    ppermute x6, waiting for transfers between devices, behind(): near = lax.ppermute(mixed, 'side', swap)  14.1 us
    pallas_call x1, Pallas kernels, key_grads(): pl.pallas_call(functools.partial(key_grads_kernel, len(keys), len(values)...  6.89 us
    ppermute x3, starting transfers between devices, send_on(): comes.append(lax.ppermute(block, 'hop', route))  6.52 us
    ppermute x6, waiting for transfers between devices, behind(): lax.ppermute(value, ('hop', 'side'), [(i, i + 2) for i in range(frames -...  6.42 us
    ppermute x6, starting transfers between devices, behind(): near = lax.ppermute(mixed, 'side', swap)  5.86 us
    pallas_call x6, Pallas kernels, picked(): pl.pallas_call(functools.partial(pick_kernel, start), in_specs=[anywhere,...  5.72 us
    ppermute x2, waiting for transfers between devices, body(): taken = lax.ppermute(sent, 'side', swap)  4.57 us
  transfers between devices with their start and end apart: 21, of which 10 were waited for; matrix products, arithmetic and copies ran while one was open for 0% of the time, Pallas kernels for 11%

commit v1 on v0

--- a/solution.py
+++ b/solution.py
@@ -74,33 +74,28 @@
     )(*[far_off(whole) for whole in wholes])
 
 
-def pick_kernel(start, far, whole, out, sem):
+def pick_kernel(far, piece, out):
     side = lax.axis_index("side")
 
     @pl.when(side == 1)
     def _():
-        copy = pltpu.make_async_copy(far, out, sem)
-        copy.start()
-        copy.wait()
+        out[...] = far[...]
 
     @pl.when(side != 1)
     def _():
-        copy = pltpu.make_async_copy(whole.at[pl.ds(start, out.shape[0])], out, sem)
-        copy.start()
-        copy.wait()
-
-
-def picked(far, whole, start):
-    anywhere = pl.BlockSpec(memory_space=pl.ANY)
-    return pl.pallas_call(
-        functools.partial(pick_kernel, start),
-        in_specs=[anywhere, anywhere],
-        out_specs=pl.BlockSpec(memory_space=pltpu.VMEM),
-        out_shape=jax.ShapeDtypeStruct(far.shape, far.dtype),
-        scratch_shapes=[pltpu.SemaphoreType.DMA],
+        out[...] = piece[...]
+
+
+def picked(far, piece):
+    vmem = pl.BlockSpec(memory_space=pltpu.VMEM)
+    return pl.pallas_call(
+        pick_kernel,
+        in_specs=[vmem, vmem],
+        out_specs=vmem,
+        out_shape=pltpu.VMEM(far.shape, far.dtype),
         compiler_params=pltpu.CompilerParams(vmem_limit_bytes=1 << 20),
         name="picked",
-    )(far, far_off(whole))
+    )(near_by(far), near_by(piece))
 
 
 def frame_index():
@@ -301,13 +296,13 @@
     first = cut_out(own[:1], (spans[:1],))
     pieces = [*first, *cut_out(own, (spans[1:], spans, spans))]
 
-    def behind(value, index):
+    def behind(value):
         far = lax.ppermute(value, ("hop", "side"), [(i, i + 2) for i in range(frames - 2)])
-        mixed = picked(far, own[index // 2], spans[index % 2][0])
+        mixed = picked(far, value)
         near = lax.ppermute(mixed, "side", swap)
         return far, near
 
-    moved = [behind(piece, index) for index, piece in enumerate(pieces)]
+    moved = [behind(piece) for piece in pieces]
     keys, values, features = (
         (whole, *zip(*moved[2 * i : 2 * i + 2])) for i, whole in enumerate(own)
     )

time: 88.6 us -> 87.6 us (0.989)
  Pallas kernels: 19.5 us -> 13.9 us
  waiting for transfers between devices: 30.7 us -> 33.3 us
  starting transfers between devices: 36.8 us -> 39 us
    pallas_call x6, Pallas kernels: 5.72 us -> 0.11 us  [picked(): pl.pallas_call(pick_kernel, in_specs=[vmem, vmem], out_specs=vmem, out_sh...]
    ppermute x6, waiting for transfers between devices: 6.42 us -> 9.53 us  [behind(): lax.ppermute(value, ('hop', 'side'), [(i, i + 2) for i in range(frames -...]
    ppermute x6, starting transfers between devices: 5.86 us -> 7.96 us  [behind(): near = lax.ppermute(mixed, 'side', swap)]
  transfers between devices with their start and end apart: 21 -> 21, of which waited for: 10 -> 10; matrix products, arithmetic and copies ran while one was open for 0% -> 0% of each run, Pallas kernels for 11% -> 5%
where the time goes in v1:
time: 87.6 us; the launch traced here: 87.3 us
  starting transfers between devices  39 us (45%)
  waiting for transfers between devices  33.3 us (38%)
  Pallas kernels  13.9 us (16%)
  between operations  1 us (1%)
    ppermute x6, starting transfers between devices, behind(): lax.ppermute(value, ('hop', 'side'), [(i, i + 2) for i in range(frames -...  19.9 us
    ppermute x6, waiting for transfers between devices, behind(): near = lax.ppermute(mixed, 'side', swap)  13.6 us
    ppermute x6, waiting for transfers between devices, behind(): lax.ppermute(value, ('hop', 'side'), [(i, i + 2) for i in range(frames -...  9.53 us
    ppermute x6, starting transfers between devices, behind(): near = lax.ppermute(mixed, 'side', swap)  7.96 us
    pallas_call x1, Pallas kernels, key_grads(): pl.pallas_call(functools.partial(key_grads_kernel, len(keys), len(values)...  6.89 us
    ppermute x3, starting transfers between devices, send_on(): comes.append(lax.ppermute(block, 'hop', route))  6.63 us
    ppermute x2, waiting for transfers between devices, body(): taken = lax.ppermute(sent, 'side', swap)  4.57 us
    ppermute x1, waiting for transfers between devices, over_clip(): terms = (mine, lax.ppermute(mine, 'set', swap))  2.85 us
  transfers between devices with their start and end apart: 21, of which 10 were waited for; matrix products, arithmetic and copies ran while one was open for 0% of the time, Pallas kernels for 5%

profile of v1, /device:TPU:0, one launch (start us, length us, event | category | flops | bytes accessed | tf_op | source)
XLA Modules:
  0.0 87.3 jit_solution(17256031464214214093)
XLA Ops:
  0.6 1.3 %cut_out.2 = (bf16[176,768]{1,0:T(8,128)(2,1)S(1)}, bf16[144,768]{1,0:T(8,128)(2,1)S(1)}, bf16[176,768]{1,0:T(8,128)(2,1)S(1)}, bf16[144,768]{1,0:T(8,128)(2,1)S(1)}, bf16[176,768]{1,0:T(8,128)(2,1)S(1)}) custom-call(bf16[320,768]{1,0:T(8,128)(2,1)} %bitcast.5, bf16[320,768]{1,0:T(8,128)(2,1)} %bitcast.10, bf16[320,768]{1,0:T(8,128)(2,1)} %bitcast.8), custom_call_target="tpu_custom_call" | custom-call | tf_op jit(solution)/shard_map/cut_out/pallas_call | solution.py:66
  2.0 5.0 %collective-permute-start.1 = (bf16[176,768]{1,0:T(8,128)(2,1)S(1)}, bf16[176,768]{1,0:T(8,128)(2,1)S(1)}, u32[]{:S(2)}, u32[]{:S(2)}) collective-permute-start(bf16[176,768]{1,0:T(8,128)(2,1)S(1)} %get-tuple-element.22.piece), channel_id=1, source_target_pairs={{0,2},{1,3},{2,4},{3,5},{4,6},{5,7},{8,10},{9,11},{10,12},{11,13},... | collective-permute-start | bytes 811016 | tf_op jit(solution)/shard_map/ppermute | solution.py:300
  7.0 3.5 %collective-permute-start = (bf16[144,768]{1,0:T(8,128)(2,1)S(1)}, bf16[144,768]{1,0:T(8,128)(2,1)S(1)}, u32[]{:S(2)}, u32[]{:S(2)}) collective-permute-start(bf16[144,768]{1,0:T(8,128)(2,1)S(1)} %get-tuple-element.21.piece), channel_id=1, source_target_pairs={{0,2},{1,3},{2,4},{3,5},{4,6},{5,7},{8,10},{9,11},{10,12},{11,13},... | collective-permute-start | bytes 663560 | tf_op jit(solution)/shard_map/ppermute | solution.py:300
  10.4 3.5 %collective-permute-start.9 = (bf16[176,768]{1,0:T(8,128)(2,1)S(1)}, bf16[176,768]{1,0:T(8,128)(2,1)S(1)}, u32[]{:S(2)}, u32[]{:S(2)}) collective-permute-start(bf16[176,768]{1,0:T(8,128)(2,1)S(1)} %get-tuple-element.25.piece), channel_id=1, source_target_pairs={{0,2},{1,3},{2,4},{3,5},{4,6},{5,7},{8,10},{9,11},{10,12},{11,13},... | collective-permute-start | bytes 811016 | tf_op jit(solution)/shard_map/ppermute | solution.py:300
  13.9 1.9 %collective-permute-start.5 = (bf16[176,768]{1,0:T(8,128)(2,1)S(1)}, bf16[176,768]{1,0:T(8,128)(2,1)S(1)}, u32[]{:S(2)}, u32[]{:S(2)}) collective-permute-start(bf16[176,768]{1,0:T(8,128)(2,1)S(1)} %get-tuple-element.23.piece), channel_id=1, source_target_pairs={{0,2},{1,3},{2,4},{3,5},{4,6},{5,7},{8,10},{9,11},{10,12},{11,13},... | collective-permute-start | bytes 811016 | tf_op jit(solution)/shard_map/ppermute | solution.py:300
  15.9 1.9 %collective-permute-start.8 = (bf16[144,768]{1,0:T(8,128)(2,1)S(1)}, bf16[144,768]{1,0:T(8,128)(2,1)S(1)}, u32[]{:S(2)}, u32[]{:S(2)}) collective-permute-start(bf16[144,768]{1,0:T(8,128)(2,1)S(1)} %get-tuple-element.24.piece), channel_id=1, source_target_pairs={{0,2},{1,3},{2,4},{3,5},{4,6},{5,7},{8,10},{9,11},{10,12},{11,13},... | collective-permute-start | bytes 663560 | tf_op jit(solution)/shard_map/ppermute | solution.py:300
  17.8 0.9 %cut_out.3.piece = bf16[144,768]{1,0:T(8,128)(2,1)S(1)} custom-call(bf16[320,768]{1,0:T(8,128)(2,1)} %bitcast.6), custom_call_target="tpu_custom_call" | custom-call | tf_op jit(solution)/shard_map/cut_out/pallas_call | solution.py:66
  18.8 4.2 %collective-permute-start.4 = (bf16[144,768]{1,0:T(8,128)(2,1)S(1)}, bf16[144,768]{1,0:T(8,128)(2,1)S(1)}, u32[]{:S(2)}, u32[]{:S(2)}) collective-permute-start(bf16[144,768]{1,0:T(8,128)(2,1)S(1)} %cut_out.3.piece), channel_id=1, source_target_pairs={{0,2},{1,3},{2,4},{3,5},{4,6},{5,7},{8,10},{9,11},{10,12},{11,13},... | collective-permute-start | bytes 663560 | tf_op jit(solution)/shard_map/ppermute | solution.py:300
  23.0 1.6 %collective-permute-start.2 = (bf16[144,768]{1,0:T(8,128)(2,1)S(1)}, bf16[144,768]{1,0:T(8,128)(2,1)S(1)}, u32[]{:S(2)}, u32[]{:S(2)}) collective-permute-start(bf16[144,768]{1,0:T(8,128)(2,1)S(1)} %picked.6), channel_id=1, source_target_pairs={{0,1},{1,0},{2,3},{3,2},{4,5},{5,4},{6,7},{7,6},{8,9},{9,8},{10,11... | collective-permute-start | bytes 663560 | tf_op jit(solution)/shard_map/ppermute | solution.py:302
  24.6 1.2 %collective-permute-start.3 = (bf16[176,768]{1,0:T(8,128)(2,1)S(1)}, bf16[176,768]{1,0:T(8,128)(2,1)S(1)}, u32[]{:S(2)}, u32[]{:S(2)}) collective-permute-start(bf16[176,768]{1,0:T(8,128)(2,1)S(1)} %picked.7), channel_id=1, source_target_pairs={{0,1},{1,0},{2,3},{3,2},{4,5},{5,4},{6,7},{7,6},{8,9},{9,8},{10,11... | collective-permute-start | bytes 811016 | tf_op jit(solution)/shard_map/ppermute | solution.py:302
  25.9 4.3 %collective-permute-done.5.far.refs_2_ = bf16[176,768]{1,0:T(8,128)(2,1)S(1)} collective-permute-done((bf16[176,768]{1,0:T(8,128)(2,1)S(1)}, bf16[176,768]{1,0:T(8,128)(2,1)S(1)}, u32[]{:S(2)}, u32[]{:S(2)}) %collective-permute-start.5) | collective-permute-done | bytes 270368 | tf_op jit(solution)/shard_map/ppermute | solution.py:300
  30.1 1.5 %collective-permute-start.11 = (bf16[176,768]{1,0:T(8,128)(2,1)S(1)}, bf16[176,768]{1,0:T(8,128)(2,1)S(1)}, u32[]{:S(2)}, u32[]{:S(2)}) collective-permute-start(bf16[176,768]{1,0:T(8,128)(2,1)S(1)} %picked.11), channel_id=1, source_target_pairs={{0,1},{1,0},{2,3},{3,2},{4,5},{5,4},{6,7},{7,6},{8,9},{9,8},{10,11... | collective-permute-start | bytes 811016 | tf_op jit(solution)/shard_map/ppermute | solution.py:302
  31.7 3.2 %collective-permute-done.8.far.refs_6_ = bf16[144,768]{1,0:T(8,128)(2,1)S(1)} collective-permute-done((bf16[144,768]{1,0:T(8,128)(2,1)S(1)}, bf16[144,768]{1,0:T(8,128)(2,1)S(1)}, u32[]{:S(2)}, u32[]{:S(2)}) %collective-permute-start.8) | collective-permute-done | bytes 221216 | tf_op jit(solution)/shard_map/ppermute | solution.py:300
  34.9 1.5 %collective-permute-start.7 = (bf16[176,768]{1,0:T(8,128)(2,1)S(1)}, bf16[176,768]{1,0:T(8,128)(2,1)S(1)}, u32[]{:S(2)}, u32[]{:S(2)}) collective-permute-start(bf16[176,768]{1,0:T(8,128)(2,1)S(1)} %picked.9), channel_id=1, source_target_pairs={{0,1},{1,0},{2,3},{3,2},{4,5},{5,4},{6,7},{7,6},{8,9},{9,8},{10,11... | collective-permute-start | bytes 811016 | tf_op jit(solution)/shard_map/ppermute | solution.py:302
  36.4 2.1 %collective-permute-done.4.far.refs_1_ = bf16[144,768]{1,0:T(8,128)(2,1)S(1)} collective-permute-done((bf16[144,768]{1,0:T(8,128)(2,1)S(1)}, bf16[144,768]{1,0:T(8,128)(2,1)S(1)}, u32[]{:S(2)}, u32[]{:S(2)}) %collective-permute-start.4) | collective-permute-done | bytes 221216 | tf_op jit(solution)/shard_map/ppermute | solution.py:300
  38.5 1.5 %collective-permute-start.10 = (bf16[144,768]{1,0:T(8,128)(2,1)S(1)}, bf16[144,768]{1,0:T(8,128)(2,1)S(1)}, u32[]{:S(2)}, u32[]{:S(2)}) collective-permute-start(bf16[144,768]{1,0:T(8,128)(2,1)S(1)} %picked.10), channel_id=1, source_target_pairs={{0,1},{1,0},{2,3},{3,2},{4,5},{5,4},{6,7},{7,6},{8,9},{9,8},{10,11... | collective-permute-start | bytes 663560 | tf_op jit(solution)/shard_map/ppermute | solution.py:302
  40.1 0.6 collective-permute-start.6
  41.2 11.2 %collective-permute-done.10.refs_8_ = bf16[144,768]{1,0:T(8,128)(2,1)S(1)} collective-permute-done((bf16[144,768]{1,0:T(8,128)(2,1)S(1)}, bf16[144,768]{1,0:T(8,128)(2,1)S(1)}, u32[]{:S(2)}, u32[]{:S(2)}) %collective-permute-start.10) | collective-permute-done | bytes 221216 | tf_op jit(solution)/shard_map/ppermute | solution.py:302
  52.4 2.4 %collective-permute-done.6.refs_3_ = bf16[144,768]{1,0:T(8,128)(2,1)S(1)} collective-permute-done((bf16[144,768]{1,0:T(8,128)(2,1)S(1)}, bf16[144,768]{1,0:T(8,128)(2,1)S(1)}, u32[]{:S(2)}, u32[]{:S(2)}) %collective-permute-start.6) | collective-permute-done | bytes 221216 | tf_op jit(solution)/shard_map/ppermute | solution.py:302
  54.9 6.9 %key_grads.1.parts = bf16[960,768]{1,0:T(8,128)(2,1)S(1)} custom-call(s32[1,8]{1,0:T(1,128)S(1)} %copy-done.8, bf16[320,768]{1,0:T(8,128)(2,1)S(1)} %bitcast.12, bf16[320,768]{1,0:T(8,128)(2,1)S(1)} %bitcast.13, bf16[320,768]{1,0:T(8,128)(2,1)S(1)} %bitcast.7, bf16[144,768]{1,0:T(8,128)(2,1)S(1)} %collective-permute-done.4.far.refs_1_, ...), custom_call_target="tpu_custom_call" | custom-call | tf_op jit(solution)/shard_map/key_grads/pallas_call | solution.py:198
  61.7 0.6 partial_gradient.5
  62.4 0.9 %partial_gradient.3 = (f32[2,2,96,384]{3,2,1,0:T(8,128)S(1)}, bf16[2,2,96,384]{3,2,1,0:T(8,128)(2,1)S(1)}) custom-call(bf16[768,640]{1,0:T(8,128)(2,1)S(1)} %turned.2.early, bf16[768,320]{1,0:T(8,128)(2,1)S(1)} %turned.3.last, bf16[960,768]{1,0:T(8,128)(2,1)S(1)} %key_grads.1.parts), custom_call_target="tpu_custom_call" | custom-call | tf_op jit(solution)/shard_map/partial_gradient/pallas_call | solution.py:266
  63.3 0.6 collective-permute-start.12
  64.6 1.6 %collective-permute-start.15 = (bf16[2,96,384]{2,1,0:T(8,128)(2,1)S(1)}, bf16[2,96,384]{2,1,0:T(8,128)(2,1)S(1)}, u32[]{:S(2)}, u32[]{:S(2)}) collective-permute-start(bf16[2,96,384]{2,1,0:T(8,128)(2,1)S(1)} %get-tuple-element.32), channel_id=1, source_target_pairs={{0,1},{1,0},{2,3},{3,2},{4,5},{5,4},{6,7},{7,6},{8,9},{9,8},{10,11... | collective-permute-start | bytes 442376 | tf_op jit(solution)/shard_map/ppermute | solution.py:328
  66.8 4.6 %collective-permute-done.15.taken = bf16[2,96,384]{2,1,0:T(8,128)(2,1)S(1)} collective-permute-done((bf16[2,96,384]{2,1,0:T(8,128)(2,1)S(1)}, bf16[2,96,384]{2,1,0:T(8,128)(2,1)S(1)}, u32[]{:S(2)}, u32[]{:S(2)}) %collective-permute-start.15) | collective-permute-done | bytes 147488 | tf_op jit(solution)/shard_map/ppermute | solution.py:328
  71.4 2.8 %collective-permute-start.16 = (bf16[96,384]{1,0:T(8,128)(2,1)S(1)}, bf16[96,384]{1,0:T(8,128)(2,1)S(1)}, u32[]{:S(2)}, u32[]{:S(2)}) collective-permute-start(bf16[96,384]{1,0:T(8,128)(2,1)S(1)} %get-tuple-element.33), channel_id=1, source_target_pairs={{0,4},{2,6},{4,0},{6,2},{1,5},{3,7},{5,1},{7,3},{8,12},{10,14},{12... | collective-permute-start | bytes 221192 | tf_op jit(solution)/shard_map/ppermute | solution.py:357
  74.5 3.6 %collective-permute-start.18 = (bf16[96,384]{1,0:T(8,128)(2,1)S(1)}, bf16[96,384]{1,0:T(8,128)(2,1)S(1)}, u32[]{:S(2)}, u32[]{:S(2)}) collective-permute-start(bf16[96,384]{1,0:T(8,128)(2,1)S(1)} %get-tuple-element.35), channel_id=1, source_target_pairs={{0,6},{2,0},{4,2},{6,4},{1,7},{3,1},{5,3},{7,5},{8,14},{10,8},{12,... | collective-permute-start | bytes 221192 | tf_op jit(solution)/shard_map/ppermute | solution.py:357
  78.4 2.1 %collective-permute-done.17.refs_1_ = bf16[96,384]{1,0:T(8,128)(2,1)S(1)} collective-permute-done((bf16[96,384]{1,0:T(8,128)(2,1)S(1)}, bf16[96,384]{1,0:T(8,128)(2,1)S(1)}, u32[]{:S(2)}, u32[]{:S(2)}) %collective-permute-start.17) | collective-permute-done | bytes 73760 | tf_op jit(solution)/shard_map/ppermute | solution.py:357
  80.5 1.6 %collective-permute-start.19 = (bf16[96,384]{1,0:T(8,128)(2,1)S(1)}, bf16[96,384]{1,0:T(8,128)(2,1)S(1)}, u32[]{:S(2)}, u32[]{:S(2)}) collective-permute-start(bf16[96,384]{1,0:T(8,128)(2,1)S(1)} %shard_map.116.first), channel_id=1, source_target_pairs={{0,16},{16,0},{1,17},{17,1},{2,18},{18,2},{3,19},{19,3},{4,20},{20... | collective-permute-start | bytes 221192 | tf_op jit(solution)/shard_map/ppermute | solution.py:416
  82.1 2.8 %collective-permute-done.19.refs_0_ = bf16[96,384]{1,0:T(8,128)(2,1)S(1)} collective-permute-done((bf16[96,384]{1,0:T(8,128)(2,1)S(1)}, bf16[96,384]{1,0:T(8,128)(2,1)S(1)}, u32[]{:S(2)}, u32[]{:S(2)}) %collective-permute-start.19) | collective-permute-done | bytes 73760 | tf_op jit(solution)/shard_map/ppermute | solution.py:416
  85.0 0.9 %shard_map.118 = (f32[96,768]{1,0:T(8,128)}, f32[96,768]{1,0:T(8,128)}, f32[96,768]{1,0:T(8,128)}) custom-call(f32[96,384]{1,0:T(8,128)S(1)} %shard_map.117.part, f32[96,768]{1,0:T(8,128)S(1)} %copy-done.3, f32[96,768]{1,0:T(8,128)S(1)} %copy-done.4, f32[96,768]{1,0:T(8,128)S(1)} %copy-done.5), custom_call_target="tpu_custom_call" | custom-call | tf_op jit(solution)/shard_map/pallas_call | solution.py:441
  86.4 0.9 %shard_map.119 = (f32[96,768]{1,0:T(8,128)}, f32[96,768]{1,0:T(8,128)}, f32[96,768]{1,0:T(8,128)}) custom-call(f32[96,384]{1,0:T(8,128)S(1)} %collective-permute-done.20.part, f32[96,768]{1,0:T(8,128)S(1)} %copy-done.3, f32[96,768]{1,0:T(8,128)S(1)} %copy-done.4, ...), custom_call_target="tpu_custom_call", output_to_operand_aliasing={{0}: (4, {}), {1}: (5, {}), {2}: (6, {})} | custom-call | tf_op jit(solution)/shard_map/pallas_call | solution.py:441
  (50 shorter events, 3.2 us)
Async XLA Ops:
  2.0 21.0 %collective-permute-start.1 = (bf16[176,768]{1,0:T(8,128)(2,1)S(1)}, bf16[176,768]{1,0:T(8,128)(2,1)S(1)}, u32[]{:S(2)}, u32[]{:S(2)}) collective-permute-start(bf16[176,768]{1,0:T(8,128)(2,1)S(1)} %get-tuple-element.22.piece), channel_id=1, source_target_pairs={{0,2},{1,3},{2,4},{3,5},{4,6},{5,7},{8,10},{9,11},{10,12},{11,13},... | collective-permute-start | bytes 811016 | tf_op jit(solution)/shard_map/ppermute | solution.py:300
  7.0 11.8 %collective-permute-start = (bf16[144,768]{1,0:T(8,128)(2,1)S(1)}, bf16[144,768]{1,0:T(8,128)(2,1)S(1)}, u32[]{:S(2)}, u32[]{:S(2)}) collective-permute-start(bf16[144,768]{1,0:T(8,128)(2,1)S(1)} %get-tuple-element.21.piece), channel_id=1, source_target_pairs={{0,2},{1,3},{2,4},{3,5},{4,6},{5,7},{8,10},{9,11},{10,12},{11,13},... | collective-permute-start | bytes 663560 | tf_op jit(solution)/shard_map/ppermute | solution.py:300
  10.4 14.2 %collective-permute-start.9 = (bf16[176,768]{1,0:T(8,128)(2,1)S(1)}, bf16[176,768]{1,0:T(8,128)(2,1)S(1)}, u32[]{:S(2)}, u32[]{:S(2)}) collective-permute-start(bf16[176,768]{1,0:T(8,128)(2,1)S(1)} %get-tuple-element.25.piece), channel_id=1, source_target_pairs={{0,2},{1,3},{2,4},{3,5},{4,6},{5,7},{8,10},{9,11},{10,12},{11,13},... | collective-permute-start | bytes 811016 | tf_op jit(solution)/shard_map/ppermute | solution.py:300
  13.9 16.2 %collective-permute-start.5 = (bf16[176,768]{1,0:T(8,128)(2,1)S(1)}, bf16[176,768]{1,0:T(8,128)(2,1)S(1)}, u32[]{:S(2)}, u32[]{:S(2)}) collective-permute-start(bf16[176,768]{1,0:T(8,128)(2,1)S(1)} %get-tuple-element.23.piece), channel_id=1, source_target_pairs={{0,2},{1,3},{2,4},{3,5},{4,6},{5,7},{8,10},{9,11},{10,12},{11,13},... | collective-permute-start | bytes 811016 | tf_op jit(solution)/shard_map/ppermute | solution.py:300
  15.9 19.0 %collective-permute-start.8 = (bf16[144,768]{1,0:T(8,128)(2,1)S(1)}, bf16[144,768]{1,0:T(8,128)(2,1)S(1)}, u32[]{:S(2)}, u32[]{:S(2)}) collective-permute-start(bf16[144,768]{1,0:T(8,128)(2,1)S(1)} %get-tuple-element.24.piece), channel_id=1, source_target_pairs={{0,2},{1,3},{2,4},{3,5},{4,6},{5,7},{8,10},{9,11},{10,12},{11,13},... | collective-permute-start | bytes 663560 | tf_op jit(solution)/shard_map/ppermute | solution.py:300
  18.8 19.7 %collective-permute-start.4 = (bf16[144,768]{1,0:T(8,128)(2,1)S(1)}, bf16[144,768]{1,0:T(8,128)(2,1)S(1)}, u32[]{:S(2)}, u32[]{:S(2)}) collective-permute-start(bf16[144,768]{1,0:T(8,128)(2,1)S(1)} %cut_out.3.piece), channel_id=1, source_target_pairs={{0,2},{1,3},{2,4},{3,5},{4,6},{5,7},{8,10},{9,11},{10,12},{11,13},... | collective-permute-start | bytes 663560 | tf_op jit(solution)/shard_map/ppermute | solution.py:300
  23.0 17.1 %collective-permute-start.2 = (bf16[144,768]{1,0:T(8,128)(2,1)S(1)}, bf16[144,768]{1,0:T(8,128)(2,1)S(1)}, u32[]{:S(2)}, u32[]{:S(2)}) collective-permute-start(bf16[144,768]{1,0:T(8,128)(2,1)S(1)} %picked.6), channel_id=1, source_target_pairs={{0,1},{1,0},{2,3},{3,2},{4,5},{5,4},{6,7},{7,6},{8,9},{9,8},{10,11... | collective-permute-start | bytes 663560 | tf_op jit(solution)/shard_map/ppermute | solution.py:302
  24.6 16.1 %copy-start.1 = (bf16[1,320,768]{2,1,0:T(8,128)(2,1)S(1)}, bf16[1,320,768]{2,1,0:T(8,128)(2,1)}, u32[]{:S(2)}) copy-start(bf16[1,320,768]{2,1,0:T(8,128)(2,1)} %param.9) | copy-start | bytes 1474564
  24.6 16.4 %collective-permute-start.3 = (bf16[176,768]{1,0:T(8,128)(2,1)S(1)}, bf16[176,768]{1,0:T(8,128)(2,1)S(1)}, u32[]{:S(2)}, u32[]{:S(2)}) collective-permute-start(bf16[176,768]{1,0:T(8,128)(2,1)S(1)} %picked.7), channel_id=1, source_target_pairs={{0,1},{1,0},{2,3},{3,2},{4,5},{5,4},{6,7},{7,6},{8,9},{9,8},{10,11... | collective-permute-start | bytes 811016 | tf_op jit(solution)/shard_map/ppermute | solution.py:302
  30.1 24.7 %collective-permute-start.11 = (bf16[176,768]{1,0:T(8,128)(2,1)S(1)}, bf16[176,768]{1,0:T(8,128)(2,1)S(1)}, u32[]{:S(2)}, u32[]{:S(2)}) collective-permute-start(bf16[176,768]{1,0:T(8,128)(2,1)S(1)} %picked.11), channel_id=1, source_target_pairs={{0,1},{1,0},{2,3},{3,2},{4,5},{5,4},{6,7},{7,6},{8,9},{9,8},{10,11... | collective-permute-start | bytes 811016 | tf_op jit(solution)/shard_map/ppermute | solution.py:302
  34.9 19.9 %collective-permute-start.7 = (bf16[176,768]{1,0:T(8,128)(2,1)S(1)}, bf16[176,768]{1,0:T(8,128)(2,1)S(1)}, u32[]{:S(2)}, u32[]{:S(2)}) collective-permute-start(bf16[176,768]{1,0:T(8,128)(2,1)S(1)} %picked.9), channel_id=1, source_target_pairs={{0,1},{1,0},{2,3},{3,2},{4,5},{5,4},{6,7},{7,6},{8,9},{9,8},{10,11... | collective-permute-start | bytes 811016 | tf_op jit(solution)/shard_map/ppermute | solution.py:302
  38.5 14.0 %collective-permute-start.10 = (bf16[144,768]{1,0:T(8,128)(2,1)S(1)}, bf16[144,768]{1,0:T(8,128)(2,1)S(1)}, u32[]{:S(2)}, u32[]{:S(2)}) collective-permute-start(bf16[144,768]{1,0:T(8,128)(2,1)S(1)} %picked.10), channel_id=1, source_target_pairs={{0,1},{1,0},{2,3},{3,2},{4,5},{5,4},{6,7},{7,6},{8,9},{9,8},{10,11... | collective-permute-start | bytes 663560 | tf_op jit(solution)/shard_map/ppermute | solution.py:302
  40.0 14.8 %copy-start = (bf16[1,320,768]{2,1,0:T(8,128)(2,1)S(1)}, bf16[1,320,768]{2,1,0:T(8,128)(2,1)}, u32[]{:S(2)}) copy-start(bf16[1,320,768]{2,1,0:T(8,128)(2,1)} %param.11) | copy-start | bytes 1474564
  40.0 14.8 %copy-start.2 = (bf16[1,320,768]{2,1,0:T(8,128)(2,1)S(1)}, bf16[1,320,768]{2,1,0:T(8,128)(2,1)}, u32[]{:S(2)}) copy-start(bf16[1,320,768]{2,1,0:T(8,128)(2,1)} %param.12) | copy-start | bytes 1474564
  40.0 14.8 %copy-start.6 = (bf16[1,320,768]{2,1,0:T(8,128)(2,1)S(1)}, bf16[1,320,768]{2,1,0:T(8,128)(2,1)}, u32[]{:S(2)}) copy-start(bf16[1,320,768]{2,1,0:T(8,128)(2,1)} %param.10) | copy-start | bytes 1474564
  40.0 14.8 %copy-start.7 = (bf16[1,320,768]{2,1,0:T(8,128)(2,1)S(1)}, bf16[1,320,768]{2,1,0:T(8,128)(2,1)}, u32[]{:S(2)}) copy-start(bf16[1,320,768]{2,1,0:T(8,128)(2,1)} %param.13) | copy-start | bytes 1474564
  40.1 14.8 %copy-start.8 = (s32[1,8]{1,0:T(1,128)S(1)}, s32[1,8]{1,0:T(1,128)}, u32[]{:S(2)}) copy-start(s32[1,8]{1,0:T(1,128)} %flags.1) | copy-start | bytes 100
  40.1 14.7 %collective-permute-start.6 = (bf16[144,768]{1,0:T(8,128)(2,1)S(1)}, bf16[144,768]{1,0:T(8,128)(2,1)S(1)}, u32[]{:S(2)}, u32[]{:S(2)}) collective-permute-start(bf16[144,768]{1,0:T(8,128)(2,1)S(1)} %picked.8), channel_id=1, source_target_pairs={{0,1},{1,0},{2,3},{3,2},{4,5},{5,4},{6,7},{7,6},{8,9},{9,8},{10,11... | collective-permute-start | bytes 663560 | tf_op jit(solution)/shard_map/ppermute | solution.py:302
  62.3 2.2 %collective-permute-start.14 = (bf16[2,2,96,384]{3,2,1,0:T(8,128)(2,1)S(1)}, bf16[2,2,96,384]{3,2,1,0:T(8,128)(2,1)S(1)}, u32[]{:S(2)}, u32[]{:S(2)}) collective-permute-start(bf16[2,2,96,384]{3,2,1,0:T(8,128)(2,1)S(1)} %partial_gradient.5), channel_id=1, source_target_pairs={{0,8},{8,0},{1,9},{9,1},{2,10},{10,2},{3,11},{11,3},{4,12},{12,4},... | collective-permute-start | bytes 884744 | tf_op jit(solution)/shard_map/ppermute | solution.py:326
  63.3 2.9 %collective-permute-start.12 = (bf16[2,2,96,384]{3,2,1,0:T(8,128)(2,1)S(1)}, bf16[2,2,96,384]{3,2,1,0:T(8,128)(2,1)S(1)}, u32[]{:S(2)}, u32[]{:S(2)}) collective-permute-start(bf16[2,2,96,384]{3,2,1,0:T(8,128)(2,1)S(1)} %get-tuple-element.27), channel_id=1, source_target_pairs={{0,8},{8,0},{1,9},{9,1},{2,10},{10,2},{3,11},{11,3},{4,12},{12,4},... | collective-permute-start | bytes 884744 | tf_op jit(solution)/shard_map/ppermute | solution.py:326
  64.6 20.4 %copy-start.3 = (f32[96,768]{1,0:T(8,128)S(1)}, f32[96,768]{1,0:T(8,128)}, u32[]{:S(2)}) copy-start(f32[96,768]{1,0:T(8,128)} %refs_0_.3) | copy-start | bytes 884740
  64.6 20.4 %copy-start.4 = (f32[96,768]{1,0:T(8,128)S(1)}, f32[96,768]{1,0:T(8,128)}, u32[]{:S(2)}) copy-start(f32[96,768]{1,0:T(8,128)} %refs_1_.3) | copy-start | bytes 884740
  64.6 20.4 %copy-start.5 = (f32[96,768]{1,0:T(8,128)S(1)}, f32[96,768]{1,0:T(8,128)}, u32[]{:S(2)}) copy-start(f32[96,768]{1,0:T(8,128)} %refs_2_.3) | copy-start | bytes 884740
  64.6 6.8 %collective-permute-start.15 = (bf16[2,96,384]{2,1,0:T(8,128)(2,1)S(1)}, bf16[2,96,384]{2,1,0:T(8,128)(2,1)S(1)}, u32[]{:S(2)}, u32[]{:S(2)}) collective-permute-start(bf16[2,96,384]{2,1,0:T(8,128)(2,1)S(1)} %get-tuple-element.32), channel_id=1, source_target_pairs={{0,1},{1,0},{2,3},{3,2},{4,5},{5,4},{6,7},{7,6},{8,9},{9,8},{10,11... | collective-permute-start | bytes 442376 | tf_op jit(solution)/shard_map/ppermute | solution.py:328
  66.3 8.2 %collective-permute-start.13 = (bf16[2,96,384]{2,1,0:T(8,128)(2,1)S(1)}, bf16[2,96,384]{2,1,0:T(8,128)(2,1)S(1)}, u32[]{:S(2)}, u32[]{:S(2)}) collective-permute-start(bf16[2,96,384]{2,1,0:T(8,128)(2,1)S(1)} %get-tuple-element.29), channel_id=1, source_target_pairs={{0,1},{1,0},{2,3},{3,2},{4,5},{5,4},{6,7},{7,6},{8,9},{9,8},{10,11... | collective-permute-start | bytes 442376 | tf_op jit(solution)/shard_map/ppermute | solution.py:328
  71.4 6.9 %collective-permute-start.16 = (bf16[96,384]{1,0:T(8,128)(2,1)S(1)}, bf16[96,384]{1,0:T(8,128)(2,1)S(1)}, u32[]{:S(2)}, u32[]{:S(2)}) collective-permute-start(bf16[96,384]{1,0:T(8,128)(2,1)S(1)} %get-tuple-element.33), channel_id=1, source_target_pairs={{0,4},{2,6},{4,0},{6,2},{1,5},{3,7},{5,1},{7,3},{8,12},{10,14},{12... | collective-permute-start | bytes 221192 | tf_op jit(solution)/shard_map/ppermute | solution.py:357
  74.2 6.3 %collective-permute-start.17 = (bf16[96,384]{1,0:T(8,128)(2,1)S(1)}, bf16[96,384]{1,0:T(8,128)(2,1)S(1)}, u32[]{:S(2)}, u32[]{:S(2)}) collective-permute-start(bf16[96,384]{1,0:T(8,128)(2,1)S(1)} %get-tuple-element.34), channel_id=1, source_target_pairs={{0,2},{2,4},{4,6},{6,0},{1,3},{3,5},{5,7},{7,1},{8,10},{10,12},{12... | collective-permute-start | bytes 221192 | tf_op jit(solution)/shard_map/ppermute | solution.py:357
  74.5 5.9 %collective-permute-start.18 = (bf16[96,384]{1,0:T(8,128)(2,1)S(1)}, bf16[96,384]{1,0:T(8,128)(2,1)S(1)}, u32[]{:S(2)}, u32[]{:S(2)}) collective-permute-start(bf16[96,384]{1,0:T(8,128)(2,1)S(1)} %get-tuple-element.35), channel_id=1, source_target_pairs={{0,6},{2,0},{4,2},{6,4},{1,7},{3,1},{5,3},{7,5},{8,14},{10,8},{12,... | collective-permute-start | bytes 221192 | tf_op jit(solution)/shard_map/ppermute | solution.py:357
  80.5 4.4 %collective-permute-start.19 = (bf16[96,384]{1,0:T(8,128)(2,1)S(1)}, bf16[96,384]{1,0:T(8,128)(2,1)S(1)}, u32[]{:S(2)}, u32[]{:S(2)}) collective-permute-start(bf16[96,384]{1,0:T(8,128)(2,1)S(1)} %shard_map.116.first), channel_id=1, source_target_pairs={{0,16},{16,0},{1,17},{17,1},{2,18},{18,2},{3,19},{19,3},{4,20},{20... | collective-permute-start | bytes 221192 | tf_op jit(solution)/shard_map/ppermute | solution.py:416
  84.9 1.4 %collective-permute-start.20 = (f32[96,384]{1,0:T(8,128)S(1)}, f32[96,384]{1,0:T(8,128)S(1)}, u32[]{:S(2)}, u32[]{:S(2)}) collective-permute-start(f32[96,384]{1,0:T(8,128)S(1)} %shard_map.117.part), channel_id=1, source_target_pairs={{0,8},{8,0},{1,9},{9,1},{2,10},{10,2},{3,11},{11,3},{4,12},{12,4},... | collective-permute-start | bytes 442376 | tf_op jit(solution)/shard_map/ppermute | solution.py:420

commit v2 on v1

--- a/solution.py
+++ b/solution.py
@@ -291,10 +291,10 @@
 
     own = (key_states[0], value_states[0], inputs[0])
     tokens = own[0].shape[0]
-    cut = tokens * 9 // 20 // 16 * 16
-    spans = ((0, cut), (cut, tokens - cut))
-    first = cut_out(own[:1], (spans[:1],))
-    pieces = [*first, *cut_out(own, (spans[1:], spans, spans))]
+    cuts = [tokens * part // 20 // 16 * 16 for part in FIRST_PIECE]
+    spans = [((0, cut), (cut, tokens - cut)) for cut in cuts]
+    first = cut_out(own[:1], (spans[0][:1],))
+    pieces = [*first, *cut_out(own, (spans[0][1:], spans[1], spans[2]))]
 
     def behind(value):
         far = lax.ppermute(value, ("hop", "side"), [(i, i + 2) for i in range(frames - 2)])
@@ -337,7 +337,7 @@
 def groups_of(hops):
     if hops > 4:
         return (tuple(range(hops)),)
-    order = (*sorted(range(1, hops), key=lambda k: -min(k, hops - k)), 0)
+    order = (*range(1, hops), 0)
     return tuple(group for group in (order[: hops // 2], order[hops // 2 :]) if group)
 
 
@@ -449,6 +449,7 @@
     )(part, *state, *outs)
 
 
+FIRST_PIECE = (9, 11, 8)
 STREAM = ("one", "two", "three", "four", "five", "six")
 
 

time: 87.6 us -> 85.5 us (0.976)
  waiting for transfers between devices: 33.3 us -> 32 us
    ppermute x6, waiting for transfers between devices: 13.6 us -> 12.3 us  [behind(): near = lax.ppermute(mixed, 'side', swap)]
    ppermute x3, starting transfers between devices: 6.63 us -> 5.72 us  [send_on(): comes.append(lax.ppermute(block, 'hop', route))]
  transfers between devices with their start and end apart: 21 -> 21, of which waited for: 10 -> 10; matrix products, arithmetic and copies ran while one was open for 0% -> 0% of each run, Pallas kernels for 5% -> 13%
where the time goes in v2:
time: 85.5 us; the launch traced here: 85.2 us
  starting transfers between devices  38.3 us (45%)
  waiting for transfers between devices  32 us (37%)
  Pallas kernels  13.9 us (16%)
  between operations  0.99 us (1%)
    ppermute x6, starting transfers between devices, behind(): lax.ppermute(value, ('hop', 'side'), [(i, i + 2) for i in range(frames -...  20.2 us
    ppermute x6, waiting for transfers between devices, behind(): near = lax.ppermute(mixed, 'side', swap)  12.3 us
    ppermute x6, waiting for transfers between devices, behind(): lax.ppermute(value, ('hop', 'side'), [(i, i + 2) for i in range(frames -...  9.24 us
    ppermute x6, starting transfers between devices, behind(): near = lax.ppermute(mixed, 'side', swap)  7.96 us
    pallas_call x1, Pallas kernels, key_grads(): pl.pallas_call(functools.partial(key_grads_kernel, len(keys), len(values)...  6.86 us
    ppermute x3, starting transfers between devices, send_on(): comes.append(lax.ppermute(block, 'hop', route))  5.72 us
    ppermute x2, waiting for transfers between devices, body(): taken = lax.ppermute(sent, 'side', swap)  4.57 us
    ppermute x1, waiting for transfers between devices, over_clip(): terms = (mine, lax.ppermute(mine, 'set', swap))  2.86 us
  transfers between devices with their start and end apart: 21, of which 10 were waited for; matrix products, arithmetic and copies ran while one was open for 0% of the time, Pallas kernels for 13%

profile of v2, /device:TPU:0, one launch (start us, length us, event | category | flops | bytes accessed | tf_op | source)
XLA Modules:
  0.0 85.2 jit_solution(10042585355610246524)
XLA Ops:
  0.6 1.3 %cut_out.2 = (bf16[176,768]{1,0:T(8,128)(2,1)S(1)}, bf16[176,768]{1,0:T(8,128)(2,1)S(1)}, bf16[144,768]{1,0:T(8,128)(2,1)S(1)}, bf16[128,768]{1,0:T(8,128)(2,1)S(1)}, bf16[192,768]{1,0:T(8,128)(2,1)S(1)}) custom-call(bf16[320,768]{1,0:T(8,128)(2,1)} %bitcast.5, bf16[320,768]{1,0:T(8,128)(2,1)} %bitcast.10, bf16[320,768]{1,0:T(8,128)(2,1)} %bitcast.8), custom_call_target="tpu_custom_call" | custom-call | tf_op jit(solution)/shard_map/cut_out/pallas_call | solution.py:66
  1.9 5.0 %collective-permute-start.1 = (bf16[192,768]{1,0:T(8,128)(2,1)S(1)}, bf16[192,768]{1,0:T(8,128)(2,1)S(1)}, u32[]{:S(2)}, u32[]{:S(2)}) collective-permute-start(bf16[192,768]{1,0:T(8,128)(2,1)S(1)} %get-tuple-element.22.piece), channel_id=1, source_target_pairs={{0,2},{1,3},{2,4},{3,5},{4,6},{5,7},{8,10},{9,11},{10,12},{11,13},... | collective-permute-start | bytes 884744 | tf_op jit(solution)/shard_map/ppermute | solution.py:300
  6.9 3.5 %collective-permute-start.9 = (bf16[144,768]{1,0:T(8,128)(2,1)S(1)}, bf16[144,768]{1,0:T(8,128)(2,1)S(1)}, u32[]{:S(2)}, u32[]{:S(2)}) collective-permute-start(bf16[144,768]{1,0:T(8,128)(2,1)S(1)} %get-tuple-element.25.piece), channel_id=1, source_target_pairs={{0,2},{1,3},{2,4},{3,5},{4,6},{5,7},{8,10},{9,11},{10,12},{11,13},... | collective-permute-start | bytes 663560 | tf_op jit(solution)/shard_map/ppermute | solution.py:300
  10.4 3.5 %collective-permute-start.8 = (bf16[176,768]{1,0:T(8,128)(2,1)S(1)}, bf16[176,768]{1,0:T(8,128)(2,1)S(1)}, u32[]{:S(2)}, u32[]{:S(2)}) collective-permute-start(bf16[176,768]{1,0:T(8,128)(2,1)S(1)} %get-tuple-element.24.piece), channel_id=1, source_target_pairs={{0,2},{1,3},{2,4},{3,5},{4,6},{5,7},{8,10},{9,11},{10,12},{11,13},... | collective-permute-start | bytes 811016 | tf_op jit(solution)/shard_map/ppermute | solution.py:300
  13.9 1.9 %collective-permute-start.5 = (bf16[176,768]{1,0:T(8,128)(2,1)S(1)}, bf16[176,768]{1,0:T(8,128)(2,1)S(1)}, u32[]{:S(2)}, u32[]{:S(2)}) collective-permute-start(bf16[176,768]{1,0:T(8,128)(2,1)S(1)} %get-tuple-element.23.piece), channel_id=1, source_target_pairs={{0,2},{1,3},{2,4},{3,5},{4,6},{5,7},{8,10},{9,11},{10,12},{11,13},... | collective-permute-start | bytes 811016 | tf_op jit(solution)/shard_map/ppermute | solution.py:300
  15.8 0.9 %cut_out.3.piece = bf16[144,768]{1,0:T(8,128)(2,1)S(1)} custom-call(bf16[320,768]{1,0:T(8,128)(2,1)} %bitcast.6), custom_call_target="tpu_custom_call" | custom-call | tf_op jit(solution)/shard_map/cut_out/pallas_call | solution.py:66
  16.8 1.9 %collective-permute-start.4 = (bf16[144,768]{1,0:T(8,128)(2,1)S(1)}, bf16[144,768]{1,0:T(8,128)(2,1)S(1)}, u32[]{:S(2)}, u32[]{:S(2)}) collective-permute-start(bf16[144,768]{1,0:T(8,128)(2,1)S(1)} %cut_out.3.piece), channel_id=1, source_target_pairs={{0,2},{1,3},{2,4},{3,5},{4,6},{5,7},{8,10},{9,11},{10,12},{11,13},... | collective-permute-start | bytes 663560 | tf_op jit(solution)/shard_map/ppermute | solution.py:300
  19.0 4.4 %collective-permute-start = (bf16[128,768]{1,0:T(8,128)(2,1)S(1)}, bf16[128,768]{1,0:T(8,128)(2,1)S(1)}, u32[]{:S(2)}, u32[]{:S(2)}) collective-permute-start(bf16[128,768]{1,0:T(8,128)(2,1)S(1)} %get-tuple-element.21.piece), channel_id=1, source_target_pairs={{0,2},{1,3},{2,4},{3,5},{4,6},{5,7},{8,10},{9,11},{10,12},{11,13},... | collective-permute-start | bytes 589832 | tf_op jit(solution)/shard_map/ppermute | solution.py:300
  23.5 1.6 %collective-permute-start.11 = (bf16[144,768]{1,0:T(8,128)(2,1)S(1)}, bf16[144,768]{1,0:T(8,128)(2,1)S(1)}, u32[]{:S(2)}, u32[]{:S(2)}) collective-permute-start(bf16[144,768]{1,0:T(8,128)(2,1)S(1)} %picked.11), channel_id=1, source_target_pairs={{0,1},{1,0},{2,3},{3,2},{4,5},{5,4},{6,7},{7,6},{8,9},{9,8},{10,11... | collective-permute-start | bytes 663560 | tf_op jit(solution)/shard_map/ppermute | solution.py:302
  25.1 1.2 %collective-permute-start.3 = (bf16[192,768]{1,0:T(8,128)(2,1)S(1)}, bf16[192,768]{1,0:T(8,128)(2,1)S(1)}, u32[]{:S(2)}, u32[]{:S(2)}) collective-permute-start(bf16[192,768]{1,0:T(8,128)(2,1)S(1)} %picked.7), channel_id=1, source_target_pairs={{0,1},{1,0},{2,3},{3,2},{4,5},{5,4},{6,7},{7,6},{8,9},{9,8},{10,11... | collective-permute-start | bytes 884744 | tf_op jit(solution)/shard_map/ppermute | solution.py:302
  26.4 4.3 %collective-permute-done.5.far.refs_2_ = bf16[176,768]{1,0:T(8,128)(2,1)S(1)} collective-permute-done((bf16[176,768]{1,0:T(8,128)(2,1)S(1)}, bf16[176,768]{1,0:T(8,128)(2,1)S(1)}, u32[]{:S(2)}, u32[]{:S(2)}) %collective-permute-start.5) | collective-permute-done | bytes 270368 | tf_op jit(solution)/shard_map/ppermute | solution.py:300
  30.6 1.5 %collective-permute-start.10 = (bf16[176,768]{1,0:T(8,128)(2,1)S(1)}, bf16[176,768]{1,0:T(8,128)(2,1)S(1)}, u32[]{:S(2)}, u32[]{:S(2)}) collective-permute-start(bf16[176,768]{1,0:T(8,128)(2,1)S(1)} %picked.10), channel_id=1, source_target_pairs={{0,1},{1,0},{2,3},{3,2},{4,5},{5,4},{6,7},{7,6},{8,9},{9,8},{10,11... | collective-permute-start | bytes 811016 | tf_op jit(solution)/shard_map/ppermute | solution.py:302
  32.2 3.1 %collective-permute-done.4.far.refs_1_ = bf16[144,768]{1,0:T(8,128)(2,1)S(1)} collective-permute-done((bf16[144,768]{1,0:T(8,128)(2,1)S(1)}, bf16[144,768]{1,0:T(8,128)(2,1)S(1)}, u32[]{:S(2)}, u32[]{:S(2)}) %collective-permute-start.4) | collective-permute-done | bytes 221216 | tf_op jit(solution)/shard_map/ppermute | solution.py:300
  35.3 1.5 %collective-permute-start.7 = (bf16[176,768]{1,0:T(8,128)(2,1)S(1)}, bf16[176,768]{1,0:T(8,128)(2,1)S(1)}, u32[]{:S(2)}, u32[]{:S(2)}) collective-permute-start(bf16[176,768]{1,0:T(8,128)(2,1)S(1)} %picked.9), channel_id=1, source_target_pairs={{0,1},{1,0},{2,3},{3,2},{4,5},{5,4},{6,7},{7,6},{8,9},{9,8},{10,11... | collective-permute-start | bytes 811016 | tf_op jit(solution)/shard_map/ppermute | solution.py:302
  36.9 1.5 %collective-permute-done.refs_1_.far = bf16[128,768]{1,0:T(8,128)(2,1)S(1)} collective-permute-done((bf16[128,768]{1,0:T(8,128)(2,1)S(1)}, bf16[128,768]{1,0:T(8,128)(2,1)S(1)}, u32[]{:S(2)}, u32[]{:S(2)}) %collective-permute-start) | collective-permute-done | bytes 196640 | tf_op jit(solution)/shard_map/ppermute | solution.py:300
  38.4 1.5 %collective-permute-start.6 = (bf16[144,768]{1,0:T(8,128)(2,1)S(1)}, bf16[144,768]{1,0:T(8,128)(2,1)S(1)}, u32[]{:S(2)}, u32[]{:S(2)}) collective-permute-start(bf16[144,768]{1,0:T(8,128)(2,1)S(1)} %picked.8), channel_id=1, source_target_pairs={{0,1},{1,0},{2,3},{3,2},{4,5},{5,4},{6,7},{7,6},{8,9},{9,8},{10,11... | collective-permute-start | bytes 663560 | tf_op jit(solution)/shard_map/ppermute | solution.py:302
  40.0 0.6 collective-permute-start.2
  40.9 12.3 %collective-permute-done.6.refs_3_ = bf16[144,768]{1,0:T(8,128)(2,1)S(1)} collective-permute-done((bf16[144,768]{1,0:T(8,128)(2,1)S(1)}, bf16[144,768]{1,0:T(8,128)(2,1)S(1)}, u32[]{:S(2)}, u32[]{:S(2)}) %collective-permute-start.6) | collective-permute-done | bytes 221216 | tf_op jit(solution)/shard_map/ppermute | solution.py:302
  53.2 6.9 %key_grads.1.parts = bf16[960,768]{1,0:T(8,128)(2,1)S(1)} custom-call(s32[1,8]{1,0:T(1,128)S(1)} %copy-done.8, bf16[320,768]{1,0:T(8,128)(2,1)S(1)} %bitcast.12, bf16[320,768]{1,0:T(8,128)(2,1)S(1)} %bitcast.13, bf16[320,768]{1,0:T(8,128)(2,1)S(1)} %bitcast.7, bf16[144,768]{1,0:T(8,128)(2,1)S(1)} %collective-permute-done.4.far.refs_1_, ...), custom_call_target="tpu_custom_call" | custom-call | tf_op jit(solution)/shard_map/key_grads/pallas_call | solution.py:198
  60.3 0.6 partial_gradient.5
  61.0 0.9 %partial_gradient.3 = (f32[2,2,96,384]{3,2,1,0:T(8,128)S(1)}, bf16[2,2,96,384]{3,2,1,0:T(8,128)(2,1)S(1)}) custom-call(bf16[768,640]{1,0:T(8,128)(2,1)S(1)} %turned.2.early, bf16[768,320]{1,0:T(8,128)(2,1)S(1)} %turned.3.last, bf16[960,768]{1,0:T(8,128)(2,1)S(1)} %key_grads.1.parts), custom_call_target="tpu_custom_call" | custom-call | tf_op jit(solution)/shard_map/partial_gradient/pallas_call | solution.py:266
  61.9 0.6 collective-permute-start.12
  63.2 1.6 %collective-permute-start.15 = (bf16[2,96,384]{2,1,0:T(8,128)(2,1)S(1)}, bf16[2,96,384]{2,1,0:T(8,128)(2,1)S(1)}, u32[]{:S(2)}, u32[]{:S(2)}) collective-permute-start(bf16[2,96,384]{2,1,0:T(8,128)(2,1)S(1)} %get-tuple-element.32), channel_id=1, source_target_pairs={{0,1},{1,0},{2,3},{3,2},{4,5},{5,4},{6,7},{7,6},{8,9},{9,8},{10,11... | collective-permute-start | bytes 442376 | tf_op jit(solution)/shard_map/ppermute | solution.py:328
  65.4 4.6 %collective-permute-done.15.taken = bf16[2,96,384]{2,1,0:T(8,128)(2,1)S(1)} collective-permute-done((bf16[2,96,384]{2,1,0:T(8,128)(2,1)S(1)}, bf16[2,96,384]{2,1,0:T(8,128)(2,1)S(1)}, u32[]{:S(2)}, u32[]{:S(2)}) %collective-permute-start.15) | collective-permute-done | bytes 147488 | tf_op jit(solution)/shard_map/ppermute | solution.py:328
  70.0 1.7 %collective-permute-start.16 = (bf16[96,384]{1,0:T(8,128)(2,1)S(1)}, bf16[96,384]{1,0:T(8,128)(2,1)S(1)}, u32[]{:S(2)}, u32[]{:S(2)}) collective-permute-start(bf16[96,384]{1,0:T(8,128)(2,1)S(1)} %get-tuple-element.33), channel_id=1, source_target_pairs={{0,2},{2,4},{4,6},{6,0},{1,3},{3,5},{5,7},{7,1},{8,10},{10,12},{12... | collective-permute-start | bytes 221192 | tf_op jit(solution)/shard_map/ppermute | solution.py:357
  71.8 1.1 %collective-permute-start.17 = (bf16[96,384]{1,0:T(8,128)(2,1)S(1)}, bf16[96,384]{1,0:T(8,128)(2,1)S(1)}, u32[]{:S(2)}, u32[]{:S(2)}) collective-permute-start(bf16[96,384]{1,0:T(8,128)(2,1)S(1)} %get-tuple-element.34), channel_id=1, source_target_pairs={{0,4},{2,6},{4,0},{6,2},{1,5},{3,7},{5,1},{7,3},{8,12},{10,14},{12... | collective-permute-start | bytes 221192 | tf_op jit(solution)/shard_map/ppermute | solution.py:357
  72.9 2.9 %collective-permute-start.18 = (bf16[96,384]{1,0:T(8,128)(2,1)S(1)}, bf16[96,384]{1,0:T(8,128)(2,1)S(1)}, u32[]{:S(2)}, u32[]{:S(2)}) collective-permute-start(bf16[96,384]{1,0:T(8,128)(2,1)S(1)} %get-tuple-element.35), channel_id=1, source_target_pairs={{0,6},{2,0},{4,2},{6,4},{1,7},{3,1},{5,3},{7,5},{8,14},{10,8},{12,... | collective-permute-start | bytes 221192 | tf_op jit(solution)/shard_map/ppermute | solution.py:357
  76.3 2.1 %collective-permute-done.17.refs_1_ = bf16[96,384]{1,0:T(8,128)(2,1)S(1)} collective-permute-done((bf16[96,384]{1,0:T(8,128)(2,1)S(1)}, bf16[96,384]{1,0:T(8,128)(2,1)S(1)}, u32[]{:S(2)}, u32[]{:S(2)}) %collective-permute-start.17) | collective-permute-done | bytes 73760 | tf_op jit(solution)/shard_map/ppermute | solution.py:357
  78.4 1.6 %collective-permute-start.19 = (bf16[96,384]{1,0:T(8,128)(2,1)S(1)}, bf16[96,384]{1,0:T(8,128)(2,1)S(1)}, u32[]{:S(2)}, u32[]{:S(2)}) collective-permute-start(bf16[96,384]{1,0:T(8,128)(2,1)S(1)} %shard_map.116.first), channel_id=1, source_target_pairs={{0,16},{16,0},{1,17},{17,1},{2,18},{18,2},{3,19},{19,3},{4,20},{20... | collective-permute-start | bytes 221192 | tf_op jit(solution)/shard_map/ppermute | solution.py:416
  80.0 2.9 %collective-permute-done.19.refs_0_ = bf16[96,384]{1,0:T(8,128)(2,1)S(1)} collective-permute-done((bf16[96,384]{1,0:T(8,128)(2,1)S(1)}, bf16[96,384]{1,0:T(8,128)(2,1)S(1)}, u32[]{:S(2)}, u32[]{:S(2)}) %collective-permute-start.19) | collective-permute-done | bytes 73760 | tf_op jit(solution)/shard_map/ppermute | solution.py:416
  82.9 0.9 %shard_map.118 = (f32[96,768]{1,0:T(8,128)}, f32[96,768]{1,0:T(8,128)}, f32[96,768]{1,0:T(8,128)}) custom-call(f32[96,384]{1,0:T(8,128)S(1)} %shard_map.117.part, f32[96,768]{1,0:T(8,128)S(1)} %copy-done.3, f32[96,768]{1,0:T(8,128)S(1)} %copy-done.4, f32[96,768]{1,0:T(8,128)S(1)} %copy-done.5), custom_call_target="tpu_custom_call" | custom-call | tf_op jit(solution)/shard_map/pallas_call | solution.py:441
  84.3 0.9 %shard_map.119 = (f32[96,768]{1,0:T(8,128)}, f32[96,768]{1,0:T(8,128)}, f32[96,768]{1,0:T(8,128)}) custom-call(f32[96,384]{1,0:T(8,128)S(1)} %collective-permute-done.20.part, f32[96,768]{1,0:T(8,128)S(1)} %copy-done.3, f32[96,768]{1,0:T(8,128)S(1)} %copy-done.4, ...), custom_call_target="tpu_custom_call", output_to_operand_aliasing={{0}: (4, {}), {1}: (5, {}), {2}: (6, {})} | custom-call | tf_op jit(solution)/shard_map/pallas_call | solution.py:441
  (50 shorter events, 3.5 us)
Async XLA Ops:
  1.9 21.5 %collective-permute-start.1 = (bf16[192,768]{1,0:T(8,128)(2,1)S(1)}, bf16[192,768]{1,0:T(8,128)(2,1)S(1)}, u32[]{:S(2)}, u32[]{:S(2)}) collective-permute-start(bf16[192,768]{1,0:T(8,128)(2,1)S(1)} %get-tuple-element.22.piece), channel_id=1, source_target_pairs={{0,2},{1,3},{2,4},{3,5},{4,6},{5,7},{8,10},{9,11},{10,12},{11,13},... | collective-permute-start | bytes 884744 | tf_op jit(solution)/shard_map/ppermute | solution.py:300
  6.9 12.1 %collective-permute-start.9 = (bf16[144,768]{1,0:T(8,128)(2,1)S(1)}, bf16[144,768]{1,0:T(8,128)(2,1)S(1)}, u32[]{:S(2)}, u32[]{:S(2)}) collective-permute-start(bf16[144,768]{1,0:T(8,128)(2,1)S(1)} %get-tuple-element.25.piece), channel_id=1, source_target_pairs={{0,2},{1,3},{2,4},{3,5},{4,6},{5,7},{8,10},{9,11},{10,12},{11,13},... | collective-permute-start | bytes 663560 | tf_op jit(solution)/shard_map/ppermute | solution.py:300
  10.4 14.7 %collective-permute-start.8 = (bf16[176,768]{1,0:T(8,128)(2,1)S(1)}, bf16[176,768]{1,0:T(8,128)(2,1)S(1)}, u32[]{:S(2)}, u32[]{:S(2)}) collective-permute-start(bf16[176,768]{1,0:T(8,128)(2,1)S(1)} %get-tuple-element.24.piece), channel_id=1, source_target_pairs={{0,2},{1,3},{2,4},{3,5},{4,6},{5,7},{8,10},{9,11},{10,12},{11,13},... | collective-permute-start | bytes 811016 | tf_op jit(solution)/shard_map/ppermute | solution.py:300
  13.9 16.7 %collective-permute-start.5 = (bf16[176,768]{1,0:T(8,128)(2,1)S(1)}, bf16[176,768]{1,0:T(8,128)(2,1)S(1)}, u32[]{:S(2)}, u32[]{:S(2)}) collective-permute-start(bf16[176,768]{1,0:T(8,128)(2,1)S(1)} %get-tuple-element.23.piece), channel_id=1, source_target_pairs={{0,2},{1,3},{2,4},{3,5},{4,6},{5,7},{8,10},{9,11},{10,12},{11,13},... | collective-permute-start | bytes 811016 | tf_op jit(solution)/shard_map/ppermute | solution.py:300
  16.8 18.6 %collective-permute-start.4 = (bf16[144,768]{1,0:T(8,128)(2,1)S(1)}, bf16[144,768]{1,0:T(8,128)(2,1)S(1)}, u32[]{:S(2)}, u32[]{:S(2)}) collective-permute-start(bf16[144,768]{1,0:T(8,128)(2,1)S(1)} %cut_out.3.piece), channel_id=1, source_target_pairs={{0,2},{1,3},{2,4},{3,5},{4,6},{5,7},{8,10},{9,11},{10,12},{11,13},... | collective-permute-start | bytes 663560 | tf_op jit(solution)/shard_map/ppermute | solution.py:300
  19.0 19.4 %collective-permute-start = (bf16[128,768]{1,0:T(8,128)(2,1)S(1)}, bf16[128,768]{1,0:T(8,128)(2,1)S(1)}, u32[]{:S(2)}, u32[]{:S(2)}) collective-permute-start(bf16[128,768]{1,0:T(8,128)(2,1)S(1)} %get-tuple-element.21.piece), channel_id=1, source_target_pairs={{0,2},{1,3},{2,4},{3,5},{4,6},{5,7},{8,10},{9,11},{10,12},{11,13},... | collective-permute-start | bytes 589832 | tf_op jit(solution)/shard_map/ppermute | solution.py:300
  23.5 16.5 %collective-permute-start.11 = (bf16[144,768]{1,0:T(8,128)(2,1)S(1)}, bf16[144,768]{1,0:T(8,128)(2,1)S(1)}, u32[]{:S(2)}, u32[]{:S(2)}) collective-permute-start(bf16[144,768]{1,0:T(8,128)(2,1)S(1)} %picked.11), channel_id=1, source_target_pairs={{0,1},{1,0},{2,3},{3,2},{4,5},{5,4},{6,7},{7,6},{8,9},{9,8},{10,11... | collective-permute-start | bytes 663560 | tf_op jit(solution)/shard_map/ppermute | solution.py:302
  25.1 15.5 %copy-start.1 = (bf16[1,320,768]{2,1,0:T(8,128)(2,1)S(1)}, bf16[1,320,768]{2,1,0:T(8,128)(2,1)}, u32[]{:S(2)}) copy-start(bf16[1,320,768]{2,1,0:T(8,128)(2,1)} %param.9) | copy-start | bytes 1474564
  25.1 35.0 %collective-permute-start.3 = (bf16[192,768]{1,0:T(8,128)(2,1)S(1)}, bf16[192,768]{1,0:T(8,128)(2,1)S(1)}, u32[]{:S(2)}, u32[]{:S(2)}) collective-permute-start(bf16[192,768]{1,0:T(8,128)(2,1)S(1)} %picked.7), channel_id=1, source_target_pairs={{0,1},{1,0},{2,3},{3,2},{4,5},{5,4},{6,7},{7,6},{8,9},{9,8},{10,11... | collective-permute-start | bytes 884744 | tf_op jit(solution)/shard_map/ppermute | solution.py:302
  30.6 22.6 %collective-permute-start.10 = (bf16[176,768]{1,0:T(8,128)(2,1)S(1)}, bf16[176,768]{1,0:T(8,128)(2,1)S(1)}, u32[]{:S(2)}, u32[]{:S(2)}) collective-permute-start(bf16[176,768]{1,0:T(8,128)(2,1)S(1)} %picked.10), channel_id=1, source_target_pairs={{0,1},{1,0},{2,3},{3,2},{4,5},{5,4},{6,7},{7,6},{8,9},{9,8},{10,11... | collective-permute-start | bytes 811016 | tf_op jit(solution)/shard_map/ppermute | solution.py:302
  32.1 21.0 %copy-start = (bf16[1,320,768]{2,1,0:T(8,128)(2,1)S(1)}, bf16[1,320,768]{2,1,0:T(8,128)(2,1)}, u32[]{:S(2)}) copy-start(bf16[1,320,768]{2,1,0:T(8,128)(2,1)} %param.11) | copy-start | bytes 1474564
  32.2 21.0 %copy-start.2 = (bf16[1,320,768]{2,1,0:T(8,128)(2,1)S(1)}, bf16[1,320,768]{2,1,0:T(8,128)(2,1)}, u32[]{:S(2)}) copy-start(bf16[1,320,768]{2,1,0:T(8,128)(2,1)} %param.12) | copy-start | bytes 1474564
  32.2 21.0 %copy-start.6 = (bf16[1,320,768]{2,1,0:T(8,128)(2,1)S(1)}, bf16[1,320,768]{2,1,0:T(8,128)(2,1)}, u32[]{:S(2)}) copy-start(bf16[1,320,768]{2,1,0:T(8,128)(2,1)} %param.10) | copy-start | bytes 1474564
  32.2 21.0 %copy-start.7 = (bf16[1,320,768]{2,1,0:T(8,128)(2,1)S(1)}, bf16[1,320,768]{2,1,0:T(8,128)(2,1)}, u32[]{:S(2)}) copy-start(bf16[1,320,768]{2,1,0:T(8,128)(2,1)} %param.13) | copy-start | bytes 1474564
  32.2 21.0 %copy-start.8 = (s32[1,8]{1,0:T(1,128)S(1)}, s32[1,8]{1,0:T(1,128)}, u32[]{:S(2)}) copy-start(s32[1,8]{1,0:T(1,128)} %flags.1) | copy-start | bytes 100
  35.3 17.8 %collective-permute-start.7 = (bf16[176,768]{1,0:T(8,128)(2,1)S(1)}, bf16[176,768]{1,0:T(8,128)(2,1)S(1)}, u32[]{:S(2)}, u32[]{:S(2)}) collective-permute-start(bf16[176,768]{1,0:T(8,128)(2,1)S(1)} %picked.9), channel_id=1, source_target_pairs={{0,1},{1,0},{2,3},{3,2},{4,5},{5,4},{6,7},{7,6},{8,9},{9,8},{10,11... | collective-permute-start | bytes 811016 | tf_op jit(solution)/shard_map/ppermute | solution.py:302
  38.4 14.8 %collective-permute-start.6 = (bf16[144,768]{1,0:T(8,128)(2,1)S(1)}, bf16[144,768]{1,0:T(8,128)(2,1)S(1)}, u32[]{:S(2)}, u32[]{:S(2)}) collective-permute-start(bf16[144,768]{1,0:T(8,128)(2,1)S(1)} %picked.8), channel_id=1, source_target_pairs={{0,1},{1,0},{2,3},{3,2},{4,5},{5,4},{6,7},{7,6},{8,9},{9,8},{10,11... | collective-permute-start | bytes 663560 | tf_op jit(solution)/shard_map/ppermute | solution.py:302
  40.0 20.1 %collective-permute-start.2 = (bf16[128,768]{1,0:T(8,128)(2,1)S(1)}, bf16[128,768]{1,0:T(8,128)(2,1)S(1)}, u32[]{:S(2)}, u32[]{:S(2)}) collective-permute-start(bf16[128,768]{1,0:T(8,128)(2,1)S(1)} %picked.6), channel_id=1, source_target_pairs={{0,1},{1,0},{2,3},{3,2},{4,5},{5,4},{6,7},{7,6},{8,9},{9,8},{10,11... | collective-permute-start | bytes 589832 | tf_op jit(solution)/shard_map/ppermute | solution.py:302
  60.9 2.2 %collective-permute-start.14 = (bf16[2,2,96,384]{3,2,1,0:T(8,128)(2,1)S(1)}, bf16[2,2,96,384]{3,2,1,0:T(8,128)(2,1)S(1)}, u32[]{:S(2)}, u32[]{:S(2)}) collective-permute-start(bf16[2,2,96,384]{3,2,1,0:T(8,128)(2,1)S(1)} %partial_gradient.5), channel_id=1, source_target_pairs={{0,8},{8,0},{1,9},{9,1},{2,10},{10,2},{3,11},{11,3},{4,12},{12,4},... | collective-permute-start | bytes 884744 | tf_op jit(solution)/shard_map/ppermute | solution.py:326
  61.9 2.9 %collective-permute-start.12 = (bf16[2,2,96,384]{3,2,1,0:T(8,128)(2,1)S(1)}, bf16[2,2,96,384]{3,2,1,0:T(8,128)(2,1)S(1)}, u32[]{:S(2)}, u32[]{:S(2)}) collective-permute-start(bf16[2,2,96,384]{3,2,1,0:T(8,128)(2,1)S(1)} %get-tuple-element.27), channel_id=1, source_target_pairs={{0,8},{8,0},{1,9},{9,1},{2,10},{10,2},{3,11},{11,3},{4,12},{12,4},... | collective-permute-start | bytes 884744 | tf_op jit(solution)/shard_map/ppermute | solution.py:326
  63.2 19.7 %copy-start.3 = (f32[96,768]{1,0:T(8,128)S(1)}, f32[96,768]{1,0:T(8,128)}, u32[]{:S(2)}) copy-start(f32[96,768]{1,0:T(8,128)} %refs_0_.3) | copy-start | bytes 884740
  63.2 19.7 %copy-start.4 = (f32[96,768]{1,0:T(8,128)S(1)}, f32[96,768]{1,0:T(8,128)}, u32[]{:S(2)}) copy-start(f32[96,768]{1,0:T(8,128)} %refs_1_.3) | copy-start | bytes 884740
  63.2 19.7 %copy-start.5 = (f32[96,768]{1,0:T(8,128)S(1)}, f32[96,768]{1,0:T(8,128)}, u32[]{:S(2)}) copy-start(f32[96,768]{1,0:T(8,128)} %refs_2_.3) | copy-start | bytes 884740
  63.2 6.8 %collective-permute-start.15 = (bf16[2,96,384]{2,1,0:T(8,128)(2,1)S(1)}, bf16[2,96,384]{2,1,0:T(8,128)(2,1)S(1)}, u32[]{:S(2)}, u32[]{:S(2)}) collective-permute-start(bf16[2,96,384]{2,1,0:T(8,128)(2,1)S(1)} %get-tuple-element.32), channel_id=1, source_target_pairs={{0,1},{1,0},{2,3},{3,2},{4,5},{5,4},{6,7},{7,6},{8,9},{9,8},{10,11... | collective-permute-start | bytes 442376 | tf_op jit(solution)/shard_map/ppermute | solution.py:328
  64.9 8.0 %collective-permute-start.13 = (bf16[2,96,384]{2,1,0:T(8,128)(2,1)S(1)}, bf16[2,96,384]{2,1,0:T(8,128)(2,1)S(1)}, u32[]{:S(2)}, u32[]{:S(2)}) collective-permute-start(bf16[2,96,384]{2,1,0:T(8,128)(2,1)S(1)} %get-tuple-element.29), channel_id=1, source_target_pairs={{0,1},{1,0},{2,3},{3,2},{4,5},{5,4},{6,7},{7,6},{8,9},{9,8},{10,11... | collective-permute-start | bytes 442376 | tf_op jit(solution)/shard_map/ppermute | solution.py:328
  70.0 6.2 %collective-permute-start.16 = (bf16[96,384]{1,0:T(8,128)(2,1)S(1)}, bf16[96,384]{1,0:T(8,128)(2,1)S(1)}, u32[]{:S(2)}, u32[]{:S(2)}) collective-permute-start(bf16[96,384]{1,0:T(8,128)(2,1)S(1)} %get-tuple-element.33), channel_id=1, source_target_pairs={{0,2},{2,4},{4,6},{6,0},{1,3},{3,5},{5,7},{7,1},{8,10},{10,12},{12... | collective-permute-start | bytes 221192 | tf_op jit(solution)/shard_map/ppermute | solution.py:357
  71.8 6.6 %collective-permute-start.17 = (bf16[96,384]{1,0:T(8,128)(2,1)S(1)}, bf16[96,384]{1,0:T(8,128)(2,1)S(1)}, u32[]{:S(2)}, u32[]{:S(2)}) collective-permute-start(bf16[96,384]{1,0:T(8,128)(2,1)S(1)} %get-tuple-element.34), channel_id=1, source_target_pairs={{0,4},{2,6},{4,0},{6,2},{1,5},{3,7},{5,1},{7,3},{8,12},{10,14},{12... | collective-permute-start | bytes 221192 | tf_op jit(solution)/shard_map/ppermute | solution.py:357
  72.9 5.4 %collective-permute-start.18 = (bf16[96,384]{1,0:T(8,128)(2,1)S(1)}, bf16[96,384]{1,0:T(8,128)(2,1)S(1)}, u32[]{:S(2)}, u32[]{:S(2)}) collective-permute-start(bf16[96,384]{1,0:T(8,128)(2,1)S(1)} %get-tuple-element.35), channel_id=1, source_target_pairs={{0,6},{2,0},{4,2},{6,4},{1,7},{3,1},{5,3},{7,5},{8,14},{10,8},{12,... | collective-permute-start | bytes 221192 | tf_op jit(solution)/shard_map/ppermute | solution.py:357
  78.4 4.4 %collective-permute-start.19 = (bf16[96,384]{1,0:T(8,128)(2,1)S(1)}, bf16[96,384]{1,0:T(8,128)(2,1)S(1)}, u32[]{:S(2)}, u32[]{:S(2)}) collective-permute-start(bf16[96,384]{1,0:T(8,128)(2,1)S(1)} %shard_map.116.first), channel_id=1, source_target_pairs={{0,16},{16,0},{1,17},{17,1},{2,18},{18,2},{3,19},{19,3},{4,20},{20... | collective-permute-start | bytes 221192 | tf_op jit(solution)/shard_map/ppermute | solution.py:416
  82.8 1.4 %collective-permute-start.20 = (f32[96,384]{1,0:T(8,128)S(1)}, f32[96,384]{1,0:T(8,128)S(1)}, u32[]{:S(2)}, u32[]{:S(2)}) collective-permute-start(f32[96,384]{1,0:T(8,128)S(1)} %shard_map.117.part), channel_id=1, source_target_pairs={{0,8},{8,0},{1,9},{9,1},{2,10},{10,2},{3,11},{11,3},{4,12},{12,4},... | collective-permute-start | bytes 442376 | tf_op jit(solution)/shard_map/ppermute | solution.py:420
